TPU v7x, 256 devices: a whole 4x4x8 slice. The times are simulated.
256 devices in a mesh: leaf: 32 (over x, y, core), front: 8 (over z).
Axes of the slice: x: 4, y: 4, z: 8, core: 2. Of those that a mesh axis runs over, the one named last changes fastest.
Arguments:
- child_updates: float32 [32768, 1024], P('leaf', 'front'), as said below
- initial_one: float32 [32768, 2048], P('leaf', 'front'), as said below
- initial_two: float32 [16384, 2048], P('leaf', 'front'), as said below
- pattern_one: int32 [16, 16, 16], replicated, may hold values 0 or 1
- pattern_two: int32 [8, 16, 16], replicated, may hold values 0 or 1
- parent_map_one: int32 [16, 2, 16], replicated, may hold values from 0 to 15, each once within a row
- parent_map_two: int32 [8, 2, 16], replicated, may hold values from 0 to 15, each once within a row
Outputs:
- factor_one: float32 [32768, 1024], P('leaf', 'front')
- factor_two: float32 [16384, 1024], P('leaf', 'front')
- schur_two: float32 [8192, 1024], P('leaf', 'front')
Inputs may be any that keep to these rules, and one draw needn't show every extreme that they name: `parent_map_one`: each row is a permutation of 0 to 15; only its first 8 entries are used. `parent_map_two`: each row is a permutation of 0 to 15; only its first 8 entries are used. `initial_one`: each 2048 x 2048 front block is symmetric, and positive definite after any symmetric block mask. `initial_two`: each 2048 x 2048 front block is symmetric, and positive definite after any symmetric block mask. `child_updates`: each 1024 x 1024 matrix is symmetric positive definite.
All inputs are finite; a program needn't handle non-finite values.
Results may differ from a plain program's by a relative error of at most 0.0003.
Values sent between devices are 32-bit elements; how exact they have to be, the bound alone decides.
No kernel may reach another device: no remote copies, remote signals or barrier semaphores. Data moves between devices by JAX's collectives and lax.ppermute only.
A program may use at most 128 MiB of HBM per device.

v0:
```python
import jax
import jax.numpy as jnp
from jax import lax
from jax.experimental import pallas as pl
from jax.experimental.pallas import tpu as pltpu
from jax.sharding import Mesh, PartitionSpec as P

BLK = 128
NB = 8
FB = 16
F32 = jnp.float32
BF16 = jnp.bfloat16
VMEM = pl.BlockSpec(memory_space=pltpu.VMEM)
SMEM = pl.BlockSpec(memory_space=pltpu.SMEM)
ANY = pl.BlockSpec(memory_space=pl.ANY)
HALF = BLK // 2
CORNER_ROWS = 2 * BLK + HALF
CHILD_ROWS = 4 * BLK + HALF
LOWER_ROWS = 4 * BLK
PARAMS = pltpu.CompilerParams(vmem_limit_bytes=58 * 1024 * 1024)
LEAF = ("x", "yh", "yl", "core")


def shape(*dims):
    return jax.ShapeDtypeStruct(dims, F32)


def packed_index(row, col):
    return col * NB - col * (col - 1) // 2 + row - col


def across(piece):
    return jnp.broadcast_to(piece, (8, BLK))


def lane_columns(rows, t):
    return [across(rows[:, 8 * t + b : 8 * t + b + 1]) for b in range(8)]


def factor_eights(rows, first, last):
    sub = lax.broadcasted_iota(jnp.int32, (8, BLK), 0)
    lane = lax.broadcasted_iota(jnp.int32, (8, BLK), 1)
    diag = jnp.zeros((8, BLK), F32)
    outs = []
    following = lane_columns(rows[first], first)
    for t in range(first, last):
        head = following
        below = {g: lane_columns(rows[g], t) for g in range(t + 1, last)}
        if t + 1 < last:
            following = lane_columns(rows[t + 1], t + 1)
        scale, weight = [], {}
        for b in range(8):
            pivot = across(head[b][b : b + 1])
            scale.append(lax.rsqrt(pivot))
            diag = jnp.where(lane == 8 * t + b, pivot * scale[b], diag)
            low = head[b] * scale[b]
            for a in range(b + 1, 8):
                weight[a, b] = across(low[a : a + 1])
                head[a] = head[a] - low * weight[a, b]
        inside = (lane >= 8 * t) & (lane < 8 * t + 8)
        pivots = []
        for b in range(8):
            unit = jnp.where(lane == 8 * t + b, 1.0, 0.0)
            row = jnp.where(inside, unit, across(rows[t][b : b + 1]))
            for a in range(b):
                row = row - weight[b, a] * pivots[a]
            pivots.append(row * scale[b])
        for g in range(t + 1, last):
            lows = []
            for b in range(8):
                column = below[g][b]
                for a in range(b):
                    column = column - lows[a] * weight[b, a]
                lows.append(column * scale[b])
            if g == t + 1:
                for b in range(8):
                    for a in range(8):
                        following[a] = following[a] - lows[b] * across(lows[b][a : a + 1])
            group = jnp.where(inside, 0.0, rows[g])
            for b in range(8):
                group = group - lows[b] * pivots[b]
            rows[g] = group
        group = pivots[7]
        for b in range(6, -1, -1):
            group = jnp.where(sub == b, pivots[b], group)
        rows[t] = group
        for a in range(1, 8):
            column = weight[a, a - 1]
            for b in range(a - 2, -1, -1):
                column = jnp.where(sub == b, weight[a, b], column)
            group = jnp.where((lane == 8 * t + a) & (sub < a), column, group)
        outs.append(group)
    return outs, diag


def factor_block(block):
    rows = [block[8 * g : 8 * g + 8] for g in range(16)]
    outs, diag = factor_eights(rows, 0, 8)
    lane = lax.broadcasted_iota(jnp.int32, (8, BLK), 1)
    row_id = lax.broadcasted_iota(jnp.int32, (BLK // 2, BLK), 0)
    col_id = lax.broadcasted_iota(jnp.int32, (BLK // 2, BLK), 1)
    left = jnp.concatenate(rows[:8], 0)
    right = jnp.where((col_id > row_id) & (col_id < BLK // 2), 0.0, left)
    left_high, left_low = halves(left)
    right_high, right_low = halves(right)
    update = lax.dot_general(
        jnp.concatenate([left_high, left_high, left_low], 0),
        jnp.concatenate([right_high, right_low, right_high], 0),
        (((0,), (0,)), ((), ())),
        preferred_element_type=F32,
    )
    for g in range(8, 16):
        rows[g] = jnp.where(lane < BLK // 2, 0.0, rows[g]) - update[8 * g : 8 * g + 8]
    more, more_diag = factor_eights(rows, 8, 16)
    full = jnp.concatenate(outs + more, 0)
    row_id = lax.broadcasted_iota(jnp.int32, (BLK, BLK), 0)
    col_id = lax.broadcasted_iota(jnp.int32, (BLK, BLK), 1)
    on_diag = jnp.broadcast_to((diag + more_diag)[0:1], (BLK, BLK))
    upper = jnp.where(col_id > row_id, full, jnp.where(col_id == row_id, on_diag, 0.0))
    return upper.T, jnp.where(col_id <= row_id, full, 0.0)


def halves(value):
    high = value.astype(BF16)
    return high, (value - high.astype(F32)).astype(BF16)


def dot_nt(left, right):
    return lax.dot_general(
        left, right, (((1,), (1,)), ((), ())), preferred_element_type=F32
    )


def dot_split(left, right):
    left_high, left_low = halves(left)
    right_high, right_low = halves(right)
    return dot_nt(
        jnp.concatenate([left_high, left_high, left_low], 1),
        jnp.concatenate([right_high, right_low, right_high], 1),
    )


def factor_corner(work, chol, inverse):
    order = NB * BLK

    def one_panel(step, carry):
        first = pl.multiple_of(step * BLK, BLK)
        lower, lower_inverse = factor_block(work[step, pl.ds(first, BLK), :])
        chol[step, pl.ds(first, BLK), :] = lower
        inverse[step] = lower_inverse
        for j in range(NB - 1):

            @pl.when(step == j)
            def _():
                start = BLK * (j + 1)
                panel = dot_split(work[j, start:, :], inverse[j])
                chol[j, start:, :] = panel
                high, low = halves(panel)
                left = jnp.concatenate([high, high, low], 1)
                right = jnp.concatenate([high, low, high], 1)
                for k in range(j + 1, NB, 2):
                    wide = min(2, NB - k)
                    top = BLK * k - start
                    update = dot_nt(left[top:], right[top : top + wide * BLK])
                    for w in range(wide):
                        work[k + w, BLK * k :, :] = (
                            work[k + w, BLK * k :, :] - update[:, w * BLK : (w + 1) * BLK]
                        )

        return carry

    for j in range(1, NB):
        chol[j, : j * BLK, :] = jnp.zeros((j * BLK, BLK), F32)
    lax.fori_loop(0, NB, one_panel, 0)


def solve_rows(right_side, chol, inverse, solved, solved_high, solved_low):
    for p in range(0, NB, 2):
        first, second = right_side(p), right_side(p + 1)
        if p:
            depth = range(p)
            left_high = jnp.concatenate([solved_high[k] for k in depth], 1)
            left_low = jnp.concatenate([solved_low[k] for k in depth], 1)
            right = jnp.concatenate([chol[k, p * BLK : (p + 2) * BLK, :] for k in depth], 1)
            right_high, right_low = halves(right)
            update = (
                dot_nt(left_high, right_high)
                + dot_nt(left_high, right_low)
                + dot_nt(left_low, right_high)
            )
            first = first - update[:, :BLK]
            second = second - update[:, BLK:]
        first = dot_split(first, inverse[p])
        second = second - dot_split(first, chol[p, (p + 1) * BLK : (p + 2) * BLK, :])
        second = dot_split(second, inverse[p + 1])
        for k, value in ((p, first), (p + 1, second)):
            solved[k] = value
            solved_high[k], solved_low[k] = halves(value)


def kept(pattern, front, row, col):
    return (pattern[front, row, col] == 1) | (pattern[front, col, row] == 1) | (row == col)


def first_turn(core, z):
    return jnp.where((core == 0) & (z >= 4), 1, 0)


def send_blocks(tile, core, z, out):
    base = NB // 2 * core
    for turn in range(2):
        local = (z + first_turn(core, z) + turn) % 4
        block = tile[local]
        at = turn * BLK

        @pl.when(base + local >= z)
        def _():
            out[at : at + BLK, :] = block

        @pl.when(base + local < z)
        def _():
            out[at : at + BLK, :] = block.T

    block = tile[(z + 2) % 4]

    @pl.when(z % 4 < 2)
    def _():
        out[2 * BLK :, :] = block[:HALF, :]

    @pl.when(z % 4 >= 2)
    def _():
        out[2 * BLK :, :] = block.T[HALF:, :]


def static_blocks():
    where = {}
    for core in range(2):
        for z in range(NB):
            turn0 = 1 if core == 0 and z >= 4 else 0
            for turn in range(2):
                row = 4 * core + (z + turn0 + turn) % 4
                where[max(row, z), min(row, z)] = [(core * NB + z, turn * BLK, BLK)]
            if z // 4 == core:
                row = 4 * core + (z + 2) % 4
                key = (max(row, z), min(row, z))
                entry = (core * NB + z, 2 * BLK, HALF)
                known = where.setdefault(key, [])
                if z % 4 < 2:
                    known.insert(0, entry)
                else:
                    known.append(entry)
    return where


def send_child(child, z, out):
    for turn in range(4):
        row = (z + turn) % NB
        at = turn * BLK
        block = child[pl.ds(pl.multiple_of(row * BLK, BLK), BLK), :]

        @pl.when(row >= z)
        def _():
            out[at : at + BLK, :] = block

        @pl.when(row < z)
        def _():
            out[at : at + BLK, :] = block.T

    row = (z + 4) % NB
    block = child[pl.ds(pl.multiple_of(row * BLK, BLK), BLK), :]

    @pl.when(row > z)
    def _():
        out[4 * BLK :, :] = block[:HALF, :]

    @pl.when(row < z)
    def _():
        out[4 * BLK :, :] = block.T[HALF:, :]


def child_copies(gathered, children, sems):
    return [
        pltpu.make_async_copy(
            gathered.at[:, :CHILD_ROWS, :], children.at[:, :CHILD_ROWS, :], sems.at[0]
        )
    ] + [
        pltpu.make_async_copy(
            gathered.at[child * NB + 4 : child * NB + 8, 4 * BLK : CHILD_ROWS, :],
            children.at[child * NB : child * NB + 4, CHILD_ROWS:, :],
            sems.at[1 + child],
        )
        for child in range(2)
    ]


def each_gathered(block_map, front, children, visit):
    def one(n, carry):
        child, m = n // 36, n % 36
        z = jnp.where(m < 32, m // 4, m - 32)
        turn = jnp.where(m < 32, m % 4, 4)
        other = (z + turn) % NB
        row = block_map[front, child, jnp.maximum(z, other)]
        col = block_map[front, child, jnp.minimum(z, other)]
        start = pl.multiple_of(turn * BLK, BLK)
        visit(row, col, lambda: children[child * NB + z, pl.ds(start, BLK), :])
        return carry

    lax.fori_loop(0, 72, one, 0)


def each_packed(block_map, front, children, visit):
    def one_child(child, carry):
        def one_col(k, carry):
            def one_row(i, carry):
                row, col = block_map[front, child, i], block_map[front, child, k]
                index = packed_index(i, k)
                visit(row, col, lambda: children[child, index])
                return carry

            return lax.fori_loop(k, NB, one_row, carry)

        return lax.fori_loop(0, NB, one_col, carry)

    lax.fori_loop(0, 2, one_child, 0)


def add_at(ref, lead, block_row, block):
    place = pl.ds(pl.multiple_of(block_row * BLK, BLK), BLK)
    ref[lead, place, :] = ref[lead, place, :] + block


def separators_into(work):
    def visit(row, col, block):
        both = (row % 2 == 0) & (col % 2 == 0)

        @pl.when(both & (row >= col))
        def _():
            add_at(work, col // 2, row // 2, block())

        @pl.when(both & (row < col))
        def _():
            add_at(work, row // 2, col // 2, block().T)

    return visit


def masked_tile(initial, pattern, front, row, local, col):
    keep = kept(pattern, front, row, col)
    return jnp.where(keep, initial[local * BLK : (local + 1) * BLK, :], 0.0)


def pack_kernel(ids, pattern_one, child, initial, merged, columns, tile, sem):
    front_one, side, z = ids[0], ids[1], ids[2]
    copy = pltpu.make_async_copy(initial.at[:, :BLK], columns, sem)
    copy.start()
    send_child(child, z, merged.at[:CHILD_ROWS, :])
    copy.wait()
    for r in range(4):
        tile[r] = masked_tile(columns, pattern_one, front_one, NB * side + 2 * r, 2 * r, 2 * z)
    send_blocks(tile, side, z, merged.at[CHILD_ROWS:, :])


def mask_kernel(
    ids,
    pattern_one,
    pattern_two,
    initial_one,
    initial_two,
    merged,
    corner_two,
    lower_two,
    row_two,
    tail_two,
    tile,
):
    front_one, side, z, front_two, sub = ids[0], ids[1], ids[2], ids[3], ids[4]
    first, second = initial_one.at[:, :BLK], initial_one.at[:, BLK:]
    for r in range(4):
        row = NB * side + 2 * r + 1
        merged[r * BLK : (r + 1) * BLK, :] = masked_tile(
            first, pattern_one, front_one, row, 2 * r + 1, 2 * z
        )
        tile[r] = masked_tile(second, pattern_one, front_one, row, 2 * r + 1, 2 * z + 1)
    send_blocks(tile, side, z, merged.at[LOWER_ROWS:, :])
    for r in range(4):
        for w in range(2):
            columns = initial_two.at[:, w * BLK : (w + 1) * BLK]
            block = masked_tile(columns, pattern_two, front_two, 4 * sub + r, r, 2 * z + w)
            at = slice(r // 2 * BLK, (r // 2 + 1) * BLK)
            if w == 0:
                (corner_two if r % 2 == 0 else lower_two)[at, :] = block
            elif r % 2 == 0:
                row_two[at, :] = block.T
            else:
                tail_two[r // 2] = block


def chol_kernel(ids, block_map, gathered, chol, inverse, work, children, sems):
    front = ids[0]
    copies = child_copies(gathered, children, sems)
    for (row, col), parts in static_blocks().items():
        start = row * BLK
        for piece, at, rows in parts:
            copies.append(
                pltpu.make_async_copy(
                    gathered.at[piece, CHILD_ROWS + at : CHILD_ROWS + at + rows, :],
                    work.at[col, start : start + rows, :],
                    sems.at[len(copies)],
                )
            )
            start += rows
    for copy in copies:
        copy.start()
    for copy in copies:
        copy.wait()
    each_gathered(block_map, front, children, separators_into(work))
    factor_corner(work, chol, inverse)


def rest_kernel(
    ids,
    block_map,
    chol,
    inverse,
    gathered,
    merged,
    factor,
    mine,
    other,
    children,
    lower,
    solved,
    solved_high,
    solved_low,
    trail,
    sems,
):
    front, side, z = ids[0], ids[1], ids[2]
    half = NB // 2 * BLK
    copies = child_copies(gathered, children, sems)
    for core in range(2):
        copies.append(
            pltpu.make_async_copy(
                merged.at[core * NB : (core + 1) * NB, :LOWER_ROWS, :],
                lower.at[:, core * half : (core + 1) * half, :],
                sems.at[3 + core],
            )
        )
    for (row, col), parts in static_blocks().items():
        start = 0
        for piece, at, rows in parts:
            copies.append(
                pltpu.make_async_copy(
                    merged.at[piece, LOWER_ROWS + at : LOWER_ROWS + at + rows, :],
                    trail.at[packed_index(row, col), start : start + rows, :],
                    sems.at[len(copies)],
                )
            )
            start += rows
    for copy in copies:
        copy.start()
    for copy in copies:
        copy.wait()

    def visit(row, col, block):
        row_odd, col_odd = row % 2 == 1, col % 2 == 1
        row_half, col_half = row // 2, col // 2

        @pl.when(row_odd & ~col_odd)
        def _():
            add_at(lower, col_half, row_half, block())

        @pl.when(~row_odd & col_odd)
        def _():
            add_at(lower, row_half, col_half, block().T)

        @pl.when(row_odd & col_odd & (row >= col))
        def _():
            add_at(trail, packed_index(row_half, col_half), 0, block())

        @pl.when(row_odd & col_odd & (row < col))
        def _():
            add_at(trail, packed_index(col_half, row_half), 0, block().T)

    each_gathered(block_map, front, children, visit)
    solve_rows(lambda k: lower[k], chol, inverse, solved, solved_high, solved_low)
    for p in range(0, NB, 2):
        high = jnp.concatenate([solved_high[k, p * BLK :, :] for k in range(NB)], 1)
        low = jnp.concatenate([solved_low[k, p * BLK :, :] for k in range(NB)], 1)
        wide_high, wide_low = high[: 2 * BLK], low[: 2 * BLK]
        update = dot_nt(high, wide_high) + dot_nt(high, wide_low) + dot_nt(low, wide_high)
        for w in range(2):
            for i in range(p + w, NB):
                index = packed_index(i, p + w)
                trail[index] = (
                    trail[index]
                    - update[(i - p) * BLK : (i - p + 1) * BLK, w * BLK : (w + 1) * BLK]
                )
    outs = [
        pltpu.make_async_copy(trail.at[pl.ds(18 * side, 18)], mine, sems.at[0]),
        pltpu.make_async_copy(trail.at[pl.ds(18 * (1 - side), 18)], other, sems.at[1]),
    ]
    for copy in outs:
        copy.start()
    for r in range(NB):
        source = solved if r % 2 else chol
        start = pl.multiple_of((side * (NB // 2) + r // 2) * BLK, BLK)
        factor[r * BLK : (r + 1) * BLK, :] = source[z, pl.ds(start, BLK), :]
    for copy in outs:
        copy.wait()


def fetch_children(side, mine, refs, children, sems):
    near_mine, near_other, far_mine, far_other = refs
    copies = []
    for n, (ref, child, half) in enumerate(
        (
            (near_mine, mine, side),
            (near_other, mine, 1 - side),
            (far_mine, 1 - mine, side),
            (far_other, 1 - mine, 1 - side),
        )
    ):
        copies.append(pltpu.make_async_copy(ref, children.at[child, pl.ds(18 * half, 18)], sems.at[n]))
        copies[-1].start()
    return copies


def chol_two_kernel(
    ids,
    block_map,
    gathered,
    near_mine,
    near_other,
    far_mine,
    far_other,
    chol,
    inverse,
    work,
    children,
    sems,
):
    side, front, sub = ids[1], ids[3], ids[4]
    copies = fetch_children(
        side, sub // 2, (near_mine, near_other, far_mine, far_other), children, sems
    )
    for core in range(2):
        for n, y in ((0, sub // 2), (1, 1 - sub // 2)):
            start = pl.multiple_of(2 * (2 * y + core) * BLK, BLK)
            copies.append(
                pltpu.make_async_copy(
                    gathered.at[core * NB : (core + 1) * NB, 2 * n * BLK : 2 * (n + 1) * BLK, :],
                    work.at[:, pl.ds(start, 2 * BLK), :],
                    sems.at[4 + 2 * core + n],
                )
            )
            copies[-1].start()
    for copy in copies:
        copy.wait()
    each_packed(block_map, front, children, separators_into(work))
    factor_corner(work, chol, inverse)


def tail_kernel(
    ids,
    map_two,
    chol,
    inverse,
    lower_near,
    rows_all,
    tail,
    near_mine,
    near_other,
    far_mine,
    far_other,
    factor,
    schur,
    children,
    lower,
    solved,
    solved_high,
    solved_low,
    trail,
    sems,
):
    side, z, front, sub = ids[1], ids[2], ids[3], ids[4]
    mine = sub // 2
    copies = fetch_children(
        side, mine, (near_mine, near_other, far_mine, far_other), children, sems
    )
    lower[:, : 2 * BLK, :] = lower_near[...]
    for s in range(4):
        for b in range(2):
            lower[2 * s + b, 2 * BLK :, :] = rows_all[s, b * BLK : (b + 1) * BLK, :]
    trail[...] = tail[...]
    for copy in copies:
        copy.wait()
    wanted = (2 * sub, 2 * sub + 1, z)

    def visit(row, col, block):
        row_half, col_half = row // 2, col // 2
        row_odd, col_odd = row % 2 == 1, col % 2 == 1
        for slot, target in enumerate(wanted):

            @pl.when(row_odd & ~col_odd & (row_half == target))
            def _():
                add_at(lower, col_half, slot, block())

            @pl.when(~row_odd & col_odd & (col_half == target))
            def _():
                add_at(lower, row_half, slot, block().T)

        for slot in range(2):

            @pl.when(row_odd & col_odd & (row_half == wanted[slot]) & (col_half == z))
            def _():
                trail[slot] = trail[slot] + block()

            @pl.when(
                row_odd & col_odd & (row != col) & (col_half == wanted[slot]) & (row_half == z)
            )
            def _():
                trail[slot] = trail[slot] + block().T

    each_packed(map_two, front, children, visit)
    solve_rows(lambda k: lower[k], chol, inverse, solved, solved_high, solved_low)
    high = jnp.concatenate([solved_high[k] for k in range(NB)], 1)
    low = jnp.concatenate([solved_low[k] for k in range(NB)], 1)
    left_high, left_low = high[: 2 * BLK], low[: 2 * BLK]
    right_high, right_low = high[2 * BLK :], low[2 * BLK :]
    update = (
        dot_nt(left_high, right_high)
        + dot_nt(left_high, right_low)
        + dot_nt(left_low, right_high)
    )
    for r in range(2):
        schur[r * BLK : (r + 1) * BLK, :] = trail[r] - update[r * BLK : (r + 1) * BLK, :]
        start = pl.multiple_of((2 * sub + r) * BLK, BLK)
        factor[2 * r * BLK : (2 * r + 1) * BLK, :] = chol[z, pl.ds(start, BLK), :]
        factor[(2 * r + 1) * BLK : (2 * r + 2) * BLK, :] = solved[z, r * BLK : (r + 1) * BLK, :]


def call(kernel, name, outs, specs, args, scratch=(), flops=0, out_specs=None):
    return pl.pallas_call(
        kernel,
        name=name,
        out_shape=outs,
        in_specs=specs,
        out_specs=out_specs or [VMEM] * len(outs),
        scratch_shapes=list(scratch),
        compiler_params=PARAMS,
        cost_estimate=pl.CostEstimate(flops=flops, bytes_accessed=flops // 400, transcendentals=0)
        if flops
        else None,
    )(*args)


def swap(value, axis):
    return lax.ppermute(value, axis, [(0, 1), (1, 0)])


def per_device(
    child_updates,
    initial_one,
    initial_two,
    pattern_one,
    pattern_two,
    parent_map_one,
    parent_map_two,
):
    x, yh, yl = lax.axis_index("x"), lax.axis_index("yh"), lax.axis_index("yl")
    core, z = lax.axis_index("core"), lax.axis_index("front")
    ids = jnp.stack([x * 4 + yh * 2 + yl, core, z, x * 2 + yh, yl * 2 + core]).astype(jnp.int32)
    panel = (NB, NB * BLK, BLK)
    block = (BLK, BLK)

    (sent,) = call(
        pack_kernel,
        "pack",
        [shape(CHILD_ROWS + CORNER_ROWS, BLK)],
        [SMEM, SMEM, VMEM, ANY],
        (ids, pattern_one, child_updates, initial_one),
        [pltpu.VMEM((NB * BLK, BLK), F32), pltpu.VMEM((4, *block), F32), pltpu.SemaphoreType.DMA],
    )
    gathered = lax.all_gather(sent, ("core", "front"), axis=0, tiled=False)
    ids_mask, _ = lax.optimization_barrier((ids, sent))
    merged, corner_two, lower_two, row_two, tail_two = call(
        mask_kernel,
        "mask",
        [
            shape(LOWER_ROWS + CORNER_ROWS, BLK),
            shape(2 * BLK, BLK),
            shape(2 * BLK, BLK),
            shape(2 * BLK, BLK),
            shape(2, *block),
        ],
        [SMEM, SMEM, SMEM, VMEM, VMEM],
        (ids_mask, pattern_one, pattern_two, initial_one, initial_two),
        [pltpu.VMEM((4, *block), F32)],
    )
    corner_two = jnp.concatenate([corner_two, swap(corner_two, "yl")], 0)
    rows_all = lax.all_gather(row_two, ("yl", "core"), axis=0, tiled=False)
    merged, gathered, corner_two, rows_all = lax.optimization_barrier(
        (merged, gathered, corner_two, rows_all)
    )
    merged_all = lax.all_gather(merged, ("core", "front"), axis=0, tiled=False)
    children_one = pltpu.VMEM((2 * NB, 5 * BLK, BLK), F32)
    chol, inverse = call(
        chol_kernel,
        "chol",
        [shape(*panel), shape(NB, *block)],
        [SMEM, SMEM, ANY],
        (ids, parent_map_one, gathered),
        [pltpu.VMEM(panel, F32), children_one, pltpu.SemaphoreType.DMA((64,))],
        flops=40_000_000_000,
    )
    lower_two, _ = lax.optimization_barrier((lower_two, gathered))
    gathered_two = lax.all_gather(corner_two, ("core", "front"), axis=0, tiled=False)
    lower_near = lax.all_gather(lower_two, "front", axis=0, tiled=False)
    factor_one, near_mine, near_other = call(
        rest_kernel,
        "rest",
        [shape(NB * BLK, BLK), shape(18, *block), shape(18, *block)],
        [SMEM, SMEM, VMEM, VMEM, ANY, ANY],
        (ids, parent_map_one, chol, inverse, gathered, merged_all),
        [children_one]
        + [pltpu.VMEM(panel, F32)] * 2
        + [pltpu.VMEM(panel, BF16)] * 2
        + [pltpu.VMEM((36, *block), F32), pltpu.SemaphoreType.DMA((64,))],
        flops=15_000_000_000,
        out_specs=[VMEM, ANY, ANY],
    )
    far_mine = swap(near_mine, "yl")
    far_other = swap(far_mine, "core")
    packed = (near_mine, near_other, far_mine, far_other)
    children = pltpu.VMEM((2, 36, *block), F32)
    chol, inverse = call(
        chol_two_kernel,
        "chol_two",
        [shape(*panel), shape(NB, *block)],
        [SMEM, SMEM] + [ANY] * 5,
        (ids, parent_map_two, gathered_two, *packed),
        [pltpu.VMEM(panel, F32), children, pltpu.SemaphoreType.DMA((8,))],
        flops=40_000_000_000,
    )
    rows = (NB, 3 * BLK, BLK)
    factor_two, schur_two = call(
        tail_kernel,
        "tail",
        [shape(4 * BLK, BLK), shape(2 * BLK, BLK)],
        [SMEM, SMEM] + [VMEM] * 5 + [ANY] * 4,
        (ids, parent_map_two, chol, inverse, lower_near, rows_all, tail_two, *packed),
        [
            children,
            pltpu.VMEM(rows, F32),
            pltpu.VMEM(rows, F32),
            pltpu.VMEM(rows, BF16),
            pltpu.VMEM(rows, BF16),
            pltpu.VMEM((2, *block), F32),
            pltpu.SemaphoreType.DMA((4,)),
        ],
    )
    return factor_one, factor_two, schur_two


def solution(mesh):
    cut = Mesh(mesh.devices.reshape(4, 2, 2, 2, 8), LEAF + ("front",))
    tile = P(LEAF, "front")
    return jax.shard_map(
        per_device,
        mesh=cut,
        in_specs=(tile, tile, tile, P(), P(), P(), P()),
        out_specs=(tile, tile, tile),
        check_vma=False,
    )
```

profile of v0, /device:TPU:1, one launch (start us, length us, event | category | flops | bytes accessed | tf_op | source)
XLA Modules:
  0.0 238.2 jit_solution(9589339018613347662)
XLA Ops:
  7.2 0.0 all-gather.10.cloned.1.call-start
  7.2 0.6 stack.23.ids
  7.8 4.7 %pack.1 = f32[896,128]{1,0:T(8,128)} custom-call(s32[5]{0:T(128)} %stack.23.ids, s32[16,16,16]{2,1,0:T(8,128)} %pattern_one.3, f32[1024,128]{1,0:T(8,128)} %child.1, f32[1024,256]{1,0:T(8,128)} %initial_one.1), custom_call_target="tpu_custom_call" | custom-call | tf_op jit(solution)/shard_map/pack/pallas_call | solution.py:644
  12.5 0.0 all-gather.10.cloned.1.call-update
  12.6 0.0 all-gather.12.cloned.1.call-start
  12.6 5.0 %mask.1 = (f32[832,128]{1,0:T(8,128)}, f32[256,128]{1,0:T(8,128)}, f32[256,128]{1,0:T(8,128)}, f32[256,128]{1,0:T(8,128)}, f32[2,128,128]{2,1,0:T(8,128)}) custom-call(s32[5]{0:T(128)} %stack.23.ids, s32[16,16,16]{2,1,0:T(8,128)} %pattern_one.3, s32[8,16,16]{2,1,0:T(8,128)} %pattern_two.1, f32[1024,256]{1,0:T(8,128)} %initial_one.1, f32[512,256]{1,0:T(8,128)} %initial_two.1), custom_call_target="tpu_custom_call" | custom-call | tf_op jit(solution)/shard_map/mask/pallas_call | solution.py:644
  17.6 2.1 collective-permute-start
  19.7 10.2 %all-gather.1 = f32[1024,128]{1,0:T(8,128)} all-gather(f32[256,128]{1,0:T(8,128)} %get-tuple-element.26), channel_id=3, replica_groups=mesh['x'=4,'yh'=2,'yl'=2,'core'=2,'front'=8] {'yl','core'}, dimensions={0}, use_global_device_ids=true | all-gather | bytes 655360 | tf_op jit(solution)/shard_map/all_gather | solution.py:702
  30.0 0.0 collective-permute-done
  30.0 1.6 pad_maximum_fusion
  31.6 36.5 %all-gather.10.cloned.1.call-done = f32[14336,128]{1,0:T(8,128)} async-done(((f32[896,128]{1,0:T(8,128)}), f32[14336,128]{1,0:T(8,128)}) %all-gather.10.cloned.1.call-update) | async-done | bytes 7340048 | tf_op jit(solution)/shard_map/all_gather | solution.py:685
  68.1 0.0 all-gather.12.cloned.1.call-update
  68.1 0.0 all-gather.14.cloned.1.call-start
  68.1 0.7 all-gather.14.cloned.1.call-update
  68.8 0.0 all-gather.16.cloned.1.call-start
  68.9 35.5 %chol.1 = (f32[8,1024,128]{2,1,0:T(8,128)}, f32[8,128,128]{2,1,0:T(8,128)}) custom-call(s32[5]{0:T(128)} %stack.23.ids, s32[16,2,16]{2,1,0:T(2,128)} %block_map.4, f32[16,896,128]{2,1,0:T(8,128)} %bitcast.12), custom_call_target="tpu_custom_call" | custom-call | flops 40000000000 | bytes 100000000 | tf_op jit(solution)/shard_map/chol/pallas_call | solution.py:644
  104.4 12.6 %all-gather.12.cloned.1.call-done = f32[13312,128]{1,0:T(8,128)} async-done(((f32[832,128]{1,0:T(8,128)}), f32[13312,128]{1,0:T(8,128)}) %all-gather.12.cloned.1.call-update) | async-done | bytes 6815760 | tf_op jit(solution)/shard_map/all_gather | solution.py:706
  117.0 30.3 %rest.1 = (f32[1024,128]{1,0:T(8,128)}, f32[18,128,128]{2,1,0:T(8,128)}, f32[18,128,128]{2,1,0:T(8,128)}) custom-call(s32[5]{0:T(128)} %stack.23.ids, s32[16,2,16]{2,1,0:T(2,128)} %block_map.4, f32[8,1024,128]{2,1,0:T(8,128)} %get-tuple-element.28.chol, f32[8,128,128]{2,1,0:T(8,128)} %get-tuple-element.29.inverse, f32[16,896,128]{2,1,0:T(8,128)} %bitcast.13, ...), custom_call_target="tpu_custom_call" | custom-call | flops 15000000512 | bytes 37500000 | tf_op jit(solution)/shard_map/rest/pallas_call | solution.py:644
  147.3 2.0 collective-permute-start.1
  149.3 26.4 %collective-permute-done.1.far_mine = f32[18,128,128]{2,1,0:T(8,128)S(1)} collective-permute-done((f32[18,128,128]{2,1,0:T(8,128)}, f32[18,128,128]{2,1,0:T(8,128)S(1)}, u32[]{:S(2)}, u32[]{:S(2)}) %collective-permute-start.1) | collective-permute-done | bytes 1179680 | tf_op jit(solution)/shard_map/ppermute | solution.py:659
  175.7 0.0 copy-start
  175.7 0.8 collective-permute-start.2
  176.5 0.0 all-gather.16.cloned.1.call-update
  176.5 0.0 all-gather.14.cloned.1.call-done
  176.5 2.4 %collective-permute-done.2.far_other = f32[18,128,128]{2,1,0:T(8,128)S(1)} collective-permute-done((f32[18,128,128]{2,1,0:T(8,128)S(1)}, f32[18,128,128]{2,1,0:T(8,128)S(1)}, u32[]{:S(2)}, u32[]{:S(2)}) %collective-permute-start.2) | collective-permute-done | bytes 1179680 | tf_op jit(solution)/shard_map/ppermute | solution.py:659
  179.0 0.0 copy-start.1
  179.0 0.0 copy-done
  179.0 1.0 copy-done.1
  180.0 34.0 %chol_two.1 = (f32[8,1024,128]{2,1,0:T(8,128)}, f32[8,128,128]{2,1,0:T(8,128)}) custom-call(s32[5]{0:T(128)} %stack.23.ids, s32[8,2,16]{2,1,0:T(2,128)} %map_two.1, f32[16,512,128]{2,1,0:T(8,128)} %bitcast.15, f32[18,128,128]{2,1,0:T(8,128)} %get-tuple-element.33.near_mine, f32[18,128,128]{2,1,0:T(8,128)} %get-tuple-element.34.near_other, ...), custom_call_target="tpu_custom_call" | custom-call | flops 40000000000 | bytes 100000000 | tf_op jit(solution)/shard_map/chol_two/pallas_call | solution.py:644
  214.0 0.0 all-gather.16.cloned.1.call-done
  214.0 17.6 %tail.1 = (f32[512,128]{1,0:T(8,128)}, f32[256,128]{1,0:T(8,128)}) custom-call(s32[5]{0:T(128)} %stack.23.ids, s32[8,2,16]{2,1,0:T(2,128)} %map_two.1, f32[8,1024,128]{2,1,0:T(8,128)} %get-tuple-element.35.chol, f32[8,128,128]{2,1,0:T(8,128)} %get-tuple-element.36.inverse, f32[8,256,128]{2,1,0:T(8,128)} %bitcast.11, f32[4,256,128]{2,1,0:T(8,128)} %bitcast.10, ...), custom_call_target="tpu_custom_call" | custom-call | tf_op jit(solution)/shard_map/tail/pallas_call | solution.py:644
Async XLA Ops:
  7.2 60.9 %all-gather.10.cloned.1.call-start = ((), (), s32[]{:S(2)}) async-start(), calls=%async_computation | async-start | bytes 7798784 | tf_op jit(solution)/shard_map/all_gather | solution.py:685
  12.6 104.4 %all-gather.12.cloned.1.call-start = ((), (), s32[]{:S(2)}) async-start(), calls=%async_computation.1 | async-start | bytes 7241728 | tf_op jit(solution)/shard_map/all_gather | solution.py:706
  17.6 12.4 %collective-permute-start = (f32[256,128]{1,0:T(8,128)}, f32[256,128]{1,0:T(8,128)S(1)}, u32[]{:S(2)}, u32[]{:S(2)}) collective-permute-start(f32[256,128]{1,0:T(8,128)} %get-tuple-element.25), channel_id=1, source_target_pairs={{0,16},{16,0},{1,17},{17,1},{2,18},{18,2},{3,19},{19,3},{4,20},{20... | collective-permute-start | bytes 393224 | tf_op jit(solution)/shard_map/ppermute | solution.py:659
  68.1 108.4 %all-gather.14.cloned.1.call-start = ((), (), s32[]{:S(2)}) async-start(), calls=%async_computation.2 | async-start | bytes 4456448 | tf_op jit(solution)/shard_map/all_gather | solution.py:718
  68.8 145.2 %all-gather.16.cloned.1.call-start = ((), (), s32[]{:S(2)}) async-start(), calls=%async_computation.3 | async-start | bytes 1179648 | tf_op jit(solution)/shard_map/all_gather | solution.py:719
  147.3 28.4 %collective-permute-start.1 = (f32[18,128,128]{2,1,0:T(8,128)}, f32[18,128,128]{2,1,0:T(8,128)S(1)}, u32[]{:S(2)}, u32[]{:S(2)}) collective-permute-start(f32[18,128,128]{2,1,0:T(8,128)} %get-tuple-element.33.near_mine), channel_id=1, source_target_pairs={{0,16},{16,0},{1,17},{17,1},{2,18},{18,2},{3,19},{19,3},{4,20},{20... | collective-permute-start | bytes 3538952 | tf_op jit(solution)/shard_map/ppermute | solution.py:659
  175.7 3.2 %copy-start = (f32[18,128,128]{2,1,0:T(8,128)}, f32[18,128,128]{2,1,0:T(8,128)S(1)}, u32[]{:S(2)}) copy-start(f32[18,128,128]{2,1,0:T(8,128)S(1)} %collective-permute-done.1.far_mine) | copy-start | bytes 3538948
  175.7 3.2 %collective-permute-start.2 = (f32[18,128,128]{2,1,0:T(8,128)S(1)}, f32[18,128,128]{2,1,0:T(8,128)S(1)}, u32[]{:S(2)}, u32[]{:S(2)}) collective-permute-start(f32[18,128,128]{2,1,0:T(8,128)S(1)} %collective-permute-done.1.far_mine), channel_id=1, source_target_pairs={{0,8},{8,0},{1,9},{9,1},{2,10},{10,2},{3,11},{11,3},{4,12},{12,4},... | collective-permute-start | bytes 3538952 | tf_op jit(solution)/shard_map/ppermute | solution.py:659
  179.0 1.0 copy-start.1
Sparse Core Ops, SparseCore 0:
  12.7 55.3 all-gather.9
  69.9 47.0 all-gather.11
  119.4 40.7 all-gather.13
  176.6 31.3 all-gather.15
where the time goes:
time: 239 us; the launch traced here: 238 us
  Pallas kernels  127 us (53%)
  waiting for transfers between devices  78.7 us (33%)
  between operations  13.8 us (6%)
  blocking collectives  10.2 us (4%)
  starting transfers between devices  5.09 us (2%)
    pallas_call x6, Pallas kernels, call(): pl.pallas_call(kernel, name=name, out_shape=outs, in_specs=specs, out_spe...  127 us
    all_gather x1, waiting for transfers between devices, per_device(): gathered = lax.all_gather(sent, ('core', 'front'), axis=0, tiled=False)  36.5 us
    ppermute x3, waiting for transfers between devices, swap(): return lax.ppermute(value, axis, [(0, 1), (1, 0)])  28.8 us
    all_gather x1, waiting for transfers between devices, per_device(): merged_all = lax.all_gather(merged, ('core', 'front'), axis=0, tiled=False)  12.6 us
    all_gather x1, blocking collectives, per_device(): rows_all = lax.all_gather(row_two, ('yl', 'core'), axis=0, tiled=False)  10.2 us
    ppermute x3, starting transfers between devices, swap(): return lax.ppermute(value, axis, [(0, 1), (1, 0)])  4.93 us
  transfers between devices with their start and end apart: 7, of which 4 were waited for; matrix products, arithmetic and copies ran while one was open for 1% of the time, Pallas kernels for 44%

commit v1 on v0

--- a/solution.py
+++ b/solution.py
@@ -176,26 +176,44 @@
 
 def solve_rows(right_side, chol, inverse, solved, solved_high, solved_low):
     for p in range(0, NB, 2):
-        first, second = right_side(p), right_side(p + 1)
+        value = right_side(p)
         if p:
             depth = range(p)
             left_high = jnp.concatenate([solved_high[k] for k in depth], 1)
             left_low = jnp.concatenate([solved_low[k] for k in depth], 1)
             right = jnp.concatenate([chol[k, p * BLK : (p + 2) * BLK, :] for k in depth], 1)
             right_high, right_low = halves(right)
-            update = (
+            value = value - (
                 dot_nt(left_high, right_high)
                 + dot_nt(left_high, right_low)
                 + dot_nt(left_low, right_high)
             )
-            first = first - update[:, :BLK]
-            second = second - update[:, BLK:]
-        first = dot_split(first, inverse[p])
-        second = second - dot_split(first, chol[p, (p + 1) * BLK : (p + 2) * BLK, :])
-        second = dot_split(second, inverse[p + 1])
-        for k, value in ((p, first), (p + 1, second)):
-            solved[k] = value
-            solved_high[k], solved_low[k] = halves(value)
+        between = chol[p, (p + 1) * BLK : (p + 2) * BLK, :]
+        corner = -dot_split(inverse[p + 1], dot_split(inverse[p].T, between))
+        pair_inverse = jnp.concatenate(
+            [
+                jnp.concatenate([inverse[p], jnp.zeros((BLK, BLK), F32)], 1),
+                jnp.concatenate([corner, inverse[p + 1]], 1),
+            ],
+            0,
+        )
+        value = dot_split(value, pair_inverse)
+        high, low = halves(value)
+        for w in range(2):
+            lanes = slice(w * BLK, (w + 1) * BLK)
+            solved[p + w] = value[:, lanes]
+            solved_high[p + w], solved_low[p + w] = high[:, lanes], low[:, lanes]
+
+
+def pair(ref, p):
+    return jnp.concatenate([ref[p], ref[p + 1]], 1)
+
+
+def place_of(block_map, front, child, slots):
+    for m in range(FB):
+        slots[child, m] = -1
+    for i in range(NB):
+        slots[child, block_map[front, child, i]] = i
 
 
 def kept(pattern, front, row, col):
@@ -308,18 +326,35 @@
     lax.fori_loop(0, 72, one, 0)
 
 
-def each_packed(block_map, front, children, visit):
+def add_packed_separators(block_map, front, children, work, evens):
     def one_child(child, carry):
-        def one_col(k, carry):
-            def one_row(i, carry):
-                row, col = block_map[front, child, i], block_map[front, child, k]
+        count = jnp.int32(0)
+        for i in range(NB):
+            evens[count] = i
+            count = count + 1 - block_map[front, child, i] % 2
+
+        def one_col(b, carry):
+            k = evens[b]
+            col = block_map[front, child, k] // 2
+
+            def one_row(a, carry):
+                i = evens[a]
+                row = block_map[front, child, i] // 2
                 index = packed_index(i, k)
-                visit(row, col, lambda: children[child, index])
+
+                @pl.when(row >= col)
+                def _():
+                    add_at(work, col, row, children[child, index])
+
+                @pl.when(row < col)
+                def _():
+                    add_at(work, row, col, children[child, index].T)
+
                 return carry
 
-            return lax.fori_loop(k, NB, one_row, carry)
-
-        return lax.fori_loop(0, NB, one_col, carry)
+            return lax.fori_loop(b, count, one_row, carry)
+
+        return lax.fori_loop(0, count, one_col, carry)
 
     lax.fori_loop(0, 2, one_child, 0)
 
@@ -329,17 +364,34 @@
     ref[lead, place, :] = ref[lead, place, :] + block
 
 
-def separators_into(work):
+def contributions_into(corner, lower, trail):
     def visit(row, col, block):
-        both = (row % 2 == 0) & (col % 2 == 0)
-
-        @pl.when(both & (row >= col))
-        def _():
-            add_at(work, col // 2, row // 2, block())
-
-        @pl.when(both & (row < col))
-        def _():
-            add_at(work, row // 2, col // 2, block().T)
+        row_odd, col_odd = row % 2 == 1, col % 2 == 1
+        row_half, col_half = row // 2, col // 2
+
+        @pl.when(~row_odd & ~col_odd & (row >= col))
+        def _():
+            add_at(corner, col_half, row_half, block())
+
+        @pl.when(~row_odd & ~col_odd & (row < col))
+        def _():
+            add_at(corner, row_half, col_half, block().T)
+
+        @pl.when(row_odd & ~col_odd)
+        def _():
+            add_at(lower, col_half, row_half, block())
+
+        @pl.when(~row_odd & col_odd)
+        def _():
+            add_at(lower, row_half, col_half, block().T)
+
+        @pl.when(row_odd & col_odd & (row >= col))
+        def _():
+            add_at(trail, packed_index(row_half, col_half), 0, block())
+
+        @pl.when(row_odd & col_odd & (row < col))
+        def _():
+            add_at(trail, packed_index(col_half, row_half), 0, block().T)
 
     return visit
 
@@ -395,7 +447,20 @@
                 tail_two[r // 2] = block
 
 
-def chol_kernel(ids, block_map, gathered, chol, inverse, work, children, sems):
+def chol_kernel(
+    ids,
+    block_map,
+    gathered,
+    chol,
+    inverse,
+    lower_out,
+    trail_out,
+    work,
+    children,
+    lower,
+    trail,
+    sems,
+):
     front = ids[0]
     copies = child_copies(gathered, children, sems)
     for (row, col), parts in static_blocks().items():
@@ -411,79 +476,88 @@
             start += rows
     for copy in copies:
         copy.start()
+    lower[...] = jnp.zeros_like(lower)
+    trail[...] = jnp.zeros_like(trail)
     for copy in copies:
         copy.wait()
-    each_gathered(block_map, front, children, separators_into(work))
+    each_gathered(block_map, front, children, contributions_into(work, lower, trail))
+    outs = [
+        pltpu.make_async_copy(lower, lower_out, sems.at[0]),
+        pltpu.make_async_copy(trail, trail_out, sems.at[1]),
+    ]
+    for copy in outs:
+        copy.start()
     factor_corner(work, chol, inverse)
+    for copy in outs:
+        copy.wait()
 
 
 def rest_kernel(
     ids,
-    block_map,
-    chol,
-    inverse,
-    gathered,
+    chol_in,
+    inverse_in,
+    lower_in,
+    trail_in,
     merged,
     factor,
     mine,
     other,
-    children,
+    chol,
+    inverse,
     lower,
+    lower_add,
     solved,
     solved_high,
     solved_low,
     trail,
+    trail_add,
     sems,
 ):
-    front, side, z = ids[0], ids[1], ids[2]
+    side, z = ids[1], ids[2]
     half = NB // 2 * BLK
-    copies = child_copies(gathered, children, sems)
-    for core in range(2):
-        copies.append(
-            pltpu.make_async_copy(
-                merged.at[core * NB : (core + 1) * NB, :LOWER_ROWS, :],
-                lower.at[:, core * half : (core + 1) * half, :],
-                sems.at[3 + core],
+    used = []
+
+    def fetch(source, target):
+        copy = pltpu.make_async_copy(source, target, sems.at[len(used)])
+        copy.start()
+        used.append(copy)
+        return copy
+
+    first = [fetch(inverse_in, inverse)]
+    columns = {}
+    for p in range(0, NB, 2):
+        columns[p] = [fetch(lower_in.at[p : p + 2], lower_add.at[p : p + 2])]
+        for core in range(2):
+            columns[p].append(
+                fetch(
+                    merged.at[core * NB + p : core * NB + p + 2, :LOWER_ROWS, :],
+                    lower.at[p : p + 2, core * half : (core + 1) * half, :],
+                )
             )
-        )
+        if p == 0:
+            first.append(fetch(chol_in, chol))
+    last = [fetch(trail_in, trail_add)]
     for (row, col), parts in static_blocks().items():
         start = 0
         for piece, at, rows in parts:
-            copies.append(
-                pltpu.make_async_copy(
+            last.append(
+                fetch(
                     merged.at[piece, LOWER_ROWS + at : LOWER_ROWS + at + rows, :],
                     trail.at[packed_index(row, col), start : start + rows, :],
-                    sems.at[len(copies)],
                 )
             )
             start += rows
-    for copy in copies:
-        copy.start()
-    for copy in copies:
+    for copy in first:
         copy.wait()
 
-    def visit(row, col, block):
-        row_odd, col_odd = row % 2 == 1, col % 2 == 1
-        row_half, col_half = row // 2, col // 2
-
-        @pl.when(row_odd & ~col_odd)
-        def _():
-            add_at(lower, col_half, row_half, block())
-
-        @pl.when(~row_odd & col_odd)
-        def _():
-            add_at(lower, row_half, col_half, block().T)
-
-        @pl.when(row_odd & col_odd & (row >= col))
-        def _():
-            add_at(trail, packed_index(row_half, col_half), 0, block())
-
-        @pl.when(row_odd & col_odd & (row < col))
-        def _():
-            add_at(trail, packed_index(col_half, row_half), 0, block().T)
-
-    each_gathered(block_map, front, children, visit)
-    solve_rows(lambda k: lower[k], chol, inverse, solved, solved_high, solved_low)
+    def right_side(p):
+        for copy in columns[p]:
+            copy.wait()
+        return pair(lower, p) + pair(lower_add, p)
+
+    solve_rows(right_side, chol, inverse, solved, solved_high, solved_low)
+    for copy in last:
+        copy.wait()
     for p in range(0, NB, 2):
         high = jnp.concatenate([solved_high[k, p * BLK :, :] for k in range(NB)], 1)
         low = jnp.concatenate([solved_low[k, p * BLK :, :] for k in range(NB)], 1)
@@ -494,6 +568,7 @@
                 index = packed_index(i, p + w)
                 trail[index] = (
                     trail[index]
+                    + trail_add[index]
                     - update[(i - p) * BLK : (i - p + 1) * BLK, w * BLK : (w + 1) * BLK]
                 )
     outs = [
@@ -538,6 +613,7 @@
     inverse,
     work,
     children,
+    evens,
     sems,
 ):
     side, front, sub = ids[1], ids[3], ids[4]
@@ -557,14 +633,14 @@
             copies[-1].start()
     for copy in copies:
         copy.wait()
-    each_packed(block_map, front, children, separators_into(work))
+    add_packed_separators(block_map, front, children, work, evens)
     factor_corner(work, chol, inverse)
 
 
 def tail_kernel(
     ids,
     map_two,
-    chol,
+    chol_in,
     inverse,
     lower_near,
     rows_all,
@@ -575,12 +651,14 @@
     far_other,
     factor,
     schur,
+    chol,
     children,
     lower,
     solved,
     solved_high,
     solved_low,
     trail,
+    slots,
     sems,
 ):
     side, z, front, sub = ids[1], ids[2], ids[3], ids[4]
@@ -588,6 +666,10 @@
     copies = fetch_children(
         side, mine, (near_mine, near_other, far_mine, far_other), children, sems
     )
+    chol_copy = pltpu.make_async_copy(chol_in, chol, sems.at[4])
+    chol_copy.start()
+    place_of(map_two, front, 0, slots)
+    place_of(map_two, front, 1, slots)
     lower[:, : 2 * BLK, :] = lower_near[...]
     for s in range(4):
         for b in range(2):
@@ -597,33 +679,44 @@
         copy.wait()
     wanted = (2 * sub, 2 * sub + 1, z)
 
-    def visit(row, col, block):
-        row_half, col_half = row // 2, col // 2
-        row_odd, col_odd = row % 2 == 1, col % 2 == 1
+    def one_child(child, carry):
         for slot, target in enumerate(wanted):
-
-            @pl.when(row_odd & ~col_odd & (row_half == target))
+            i = slots[child, 2 * target + 1]
+
+            def one_block(k, carry):
+                col = map_two[front, child, k]
+                index = packed_index(jnp.maximum(i, k), jnp.minimum(i, k))
+
+                @pl.when((col % 2 == 0) & (i > k))
+                def _():
+                    add_at(lower, col // 2, slot, children[child, index])
+
+                @pl.when((col % 2 == 0) & (i < k))
+                def _():
+                    add_at(lower, col // 2, slot, children[child, index].T)
+
+                return carry
+
+            lax.fori_loop(0, jnp.where(i >= 0, NB, 0), one_block, 0)
+        k = slots[child, 2 * z + 1]
+        for slot in range(2):
+            i = slots[child, 2 * wanted[slot] + 1]
+            both = (i >= 0) & (k >= 0)
+            index = jnp.where(both, packed_index(jnp.maximum(i, k), jnp.minimum(i, k)), 0)
+
+            @pl.when(both & (i >= k))
             def _():
-                add_at(lower, col_half, slot, block())
-
-            @pl.when(~row_odd & col_odd & (col_half == target))
+                trail[slot] = trail[slot] + children[child, index]
+
+            @pl.when(both & (i < k))
             def _():
-                add_at(lower, row_half, slot, block().T)
-
-        for slot in range(2):
-
-            @pl.when(row_odd & col_odd & (row_half == wanted[slot]) & (col_half == z))
-            def _():
-                trail[slot] = trail[slot] + block()
-
-            @pl.when(
-                row_odd & col_odd & (row != col) & (col_half == wanted[slot]) & (row_half == z)
-            )
-            def _():
-                trail[slot] = trail[slot] + block().T
-
-    each_packed(map_two, front, children, visit)
-    solve_rows(lambda k: lower[k], chol, inverse, solved, solved_high, solved_low)
+                trail[slot] = trail[slot] + children[child, index].T
+
+        return carry
+
+    lax.fori_loop(0, 2, one_child, 0)
+    chol_copy.wait()
+    solve_rows(lambda p: pair(lower, p), chol, inverse, solved, solved_high, solved_low)
     high = jnp.concatenate([solved_high[k] for k in range(NB)], 1)
     low = jnp.concatenate([solved_low[k] for k in range(NB)], 1)
     left_high, left_low = high[: 2 * BLK], low[: 2 * BLK]
@@ -704,15 +797,21 @@
         (merged, gathered, corner_two, rows_all)
     )
     merged_all = lax.all_gather(merged, ("core", "front"), axis=0, tiled=False)
-    children_one = pltpu.VMEM((2 * NB, 5 * BLK, BLK), F32)
-    chol, inverse = call(
+    chol, inverse, lower_add, trail_add = call(
         chol_kernel,
         "chol",
-        [shape(*panel), shape(NB, *block)],
+        [shape(*panel), shape(NB, *block), shape(*panel), shape(36, *block)],
         [SMEM, SMEM, ANY],
         (ids, parent_map_one, gathered),
-        [pltpu.VMEM(panel, F32), children_one, pltpu.SemaphoreType.DMA((64,))],
+        [
+            pltpu.VMEM(panel, F32),
+            pltpu.VMEM((2 * NB, 5 * BLK, BLK), F32),
+            pltpu.VMEM(panel, F32),
+            pltpu.VMEM((36, *block), F32),
+            pltpu.SemaphoreType.DMA((64,)),
+        ],
         flops=40_000_000_000,
+        out_specs=[VMEM, VMEM, ANY, ANY],
     )
     lower_two, _ = lax.optimization_barrier((lower_two, gathered))
     gathered_two = lax.all_gather(corner_two, ("core", "front"), axis=0, tiled=False)
@@ -721,12 +820,13 @@
         rest_kernel,
         "rest",
         [shape(NB * BLK, BLK), shape(18, *block), shape(18, *block)],
-        [SMEM, SMEM, VMEM, VMEM, ANY, ANY],
-        (ids, parent_map_one, chol, inverse, gathered, merged_all),
-        [children_one]
-        + [pltpu.VMEM(panel, F32)] * 2
+        [SMEM] + [ANY] * 5,
+        (ids, chol, inverse, lower_add, trail_add, merged_all),
+        [pltpu.VMEM(panel, F32), pltpu.VMEM((NB, *block), F32)]
+        + [pltpu.VMEM(panel, F32)] * 3
         + [pltpu.VMEM(panel, BF16)] * 2
-        + [pltpu.VMEM((36, *block), F32), pltpu.SemaphoreType.DMA((64,))],
+        + [pltpu.VMEM((36, *block), F32)] * 2
+        + [pltpu.SemaphoreType.DMA((64,))],
         flops=15_000_000_000,
         out_specs=[VMEM, ANY, ANY],
     )
@@ -740,7 +840,12 @@
         [shape(*panel), shape(NB, *block)],
         [SMEM, SMEM] + [ANY] * 5,
         (ids, parent_map_two, gathered_two, *packed),
-        [pltpu.VMEM(panel, F32), children, pltpu.SemaphoreType.DMA((8,))],
+        [
+            pltpu.VMEM(panel, F32),
+            children,
+            pltpu.SMEM((NB + 1,), jnp.int32),
+            pltpu.SemaphoreType.DMA((8,)),
+        ],
         flops=40_000_000_000,
     )
     rows = (NB, 3 * BLK, BLK)
@@ -748,16 +853,18 @@
         tail_kernel,
         "tail",
         [shape(4 * BLK, BLK), shape(2 * BLK, BLK)],
-        [SMEM, SMEM] + [VMEM] * 5 + [ANY] * 4,
+        [SMEM, SMEM, ANY] + [VMEM] * 4 + [ANY] * 4,
         (ids, parent_map_two, chol, inverse, lower_near, rows_all, tail_two, *packed),
         [
+            pltpu.VMEM(panel, F32),
             children,
             pltpu.VMEM(rows, F32),
             pltpu.VMEM(rows, F32),
             pltpu.VMEM(rows, BF16),
             pltpu.VMEM(rows, BF16),
             pltpu.VMEM((2, *block), F32),
-            pltpu.SemaphoreType.DMA((4,)),
+            pltpu.SMEM((2, FB), jnp.int32),
+            pltpu.SemaphoreType.DMA((5,)),
         ],
     )
     return factor_one, factor_two, schur_two

time: 239 us -> 221 us (0.925)
  Pallas kernels: 127 us -> 114 us
  waiting for transfers between devices: 78.7 us -> 73.9 us
    pallas_call x6, Pallas kernels: 127 us -> 114 us  [call(): pl.pallas_call(kernel, name=name, out_shape=outs, in_specs=specs, out_spe...]
    all_gather x1, waiting for transfers between devices: 12.6 us -> 7.97 us  [per_device(): merged_all = lax.all_gather(merged, ('core', 'front'), axis=0, tiled=False)]
  transfers between devices with their start and end apart: 7 -> 7, of which waited for: 4 -> 4; matrix products, arithmetic and copies ran while one was open for 1% -> 1% of each run, Pallas kernels for 44% -> 45%
where the time goes in v1:
time: 221 us; the launch traced here: 220 us
  Pallas kernels  114 us (52%)
  waiting for transfers between devices  73.9 us (33%)
  between operations  13.8 us (6%)
  blocking collectives  10.2 us (5%)
  starting transfers between devices  4.66 us (2%)
    pallas_call x6, Pallas kernels, call(): pl.pallas_call(kernel, name=name, out_shape=outs, in_specs=specs, out_spe...  114 us
    all_gather x1, waiting for transfers between devices, per_device(): gathered = lax.all_gather(sent, ('core', 'front'), axis=0, tiled=False)  36.5 us
    ppermute x3, waiting for transfers between devices, swap(): return lax.ppermute(value, axis, [(0, 1), (1, 0)])  28.7 us
    all_gather x1, blocking collectives, per_device(): rows_all = lax.all_gather(row_two, ('yl', 'core'), axis=0, tiled=False)  10.2 us
    all_gather x1, waiting for transfers between devices, per_device(): merged_all = lax.all_gather(merged, ('core', 'front'), axis=0, tiled=False)  7.97 us
    ppermute x3, starting transfers between devices, swap(): return lax.ppermute(value, axis, [(0, 1), (1, 0)])  4.5 us
  transfers between devices with their start and end apart: 7, of which 4 were waited for; matrix products, arithmetic and copies ran while one was open for 1% of the time, Pallas kernels for 45%

profile of v1, /device:TPU:1, one launch (start us, length us, event | category | flops | bytes accessed | tf_op | source)
XLA Modules:
  0.0 219.8 jit_solution(16477984749811880901)
XLA Ops:
  7.2 0.0 all-gather.10.cloned.1.call-start
  7.2 0.7 stack.23.ids
  7.9 4.7 %pack.1 = f32[896,128]{1,0:T(8,128)} custom-call(s32[5]{0:T(128)} %stack.23.ids, s32[16,16,16]{2,1,0:T(8,128)} %pattern_one.3, f32[1024,128]{1,0:T(8,128)} %child.1, f32[1024,256]{1,0:T(8,128)} %initial_one.1), custom_call_target="tpu_custom_call" | custom-call | tf_op jit(solution)/shard_map/pack/pallas_call | solution.py:737
  12.6 0.0 all-gather.10.cloned.1.call-update
  12.6 0.0 all-gather.12.cloned.1.call-start
  12.7 5.0 %mask.1 = (f32[832,128]{1,0:T(8,128)}, f32[256,128]{1,0:T(8,128)}, f32[256,128]{1,0:T(8,128)}, f32[256,128]{1,0:T(8,128)}, f32[2,128,128]{2,1,0:T(8,128)}) custom-call(s32[5]{0:T(128)} %stack.23.ids, s32[16,16,16]{2,1,0:T(8,128)} %pattern_one.3, s32[8,16,16]{2,1,0:T(8,128)} %pattern_two.1, f32[1024,256]{1,0:T(8,128)} %initial_one.1, f32[512,256]{1,0:T(8,128)} %initial_two.1), custom_call_target="tpu_custom_call" | custom-call | tf_op jit(solution)/shard_map/mask/pallas_call | solution.py:737
  17.7 2.1 collective-permute-start
  19.8 10.2 %all-gather.1 = f32[1024,128]{1,0:T(8,128)} all-gather(f32[256,128]{1,0:T(8,128)} %get-tuple-element.28), channel_id=3, replica_groups=mesh['x'=4,'yh'=2,'yl'=2,'core'=2,'front'=8] {'yl','core'}, dimensions={0}, use_global_device_ids=true | all-gather | bytes 655360 | tf_op jit(solution)/shard_map/all_gather | solution.py:795
  30.0 0.0 collective-permute-done
  30.0 1.6 pad_maximum_fusion
  31.7 36.5 %all-gather.10.cloned.1.call-done = f32[14336,128]{1,0:T(8,128)} async-done(((f32[896,128]{1,0:T(8,128)}), f32[14336,128]{1,0:T(8,128)}) %all-gather.10.cloned.1.call-update) | async-done | bytes 7340048 | tf_op jit(solution)/shard_map/all_gather | solution.py:778
  68.1 0.0 all-gather.12.cloned.1.call-update
  68.2 0.0 all-gather.14.cloned.1.call-start
  68.2 0.7 all-gather.14.cloned.1.call-update
  68.9 0.0 all-gather.16.cloned.1.call-start
  68.9 40.2 %chol.1 = (f32[8,1024,128]{2,1,0:T(8,128)}, f32[8,128,128]{2,1,0:T(8,128)}, f32[8,1024,128]{2,1,0:T(8,128)}, f32[36,128,128]{2,1,0:T(8,128)}) custom-call(s32[5]{0:T(128)} %stack.23.ids, s32[16,2,16]{2,1,0:T(2,128)} %block_map.2, f32[16,896,128]{2,1,0:T(8,128)} %bitcast.12), custom_call_target="tpu_custom_call" | custom-call | flops 40000000000 | bytes 100000000 | tf_op jit(solution)/shard_map/chol/pallas_call | solution.py:737
  109.1 8.0 %all-gather.12.cloned.1.call-done = f32[13312,128]{1,0:T(8,128)} async-done(((f32[832,128]{1,0:T(8,128)}), f32[13312,128]{1,0:T(8,128)}) %all-gather.12.cloned.1.call-update) | async-done | bytes 6815760 | tf_op jit(solution)/shard_map/all_gather | solution.py:799
  117.1 20.7 %rest.1 = (f32[1024,128]{1,0:T(8,128)}, f32[18,128,128]{2,1,0:T(8,128)}, f32[18,128,128]{2,1,0:T(8,128)}) custom-call(s32[5]{0:T(128)} %stack.23.ids, f32[8,1024,128]{2,1,0:T(8,128)} %get-tuple-element.30.chol_in, f32[8,128,128]{2,1,0:T(8,128)} %get-tuple-element.31.inverse_in, f32[8,1024,128]{2,1,0:T(8,128)} %get-tuple-element.32.lower_in, ...), custom_call_target="tpu_custom_call" | custom-call | flops 15000000512 | bytes 37500000 | tf_op jit(solution)/shard_map/rest/pallas_call | solution.py:737
  137.8 1.3 collective-permute-start.1
  139.1 26.3 %collective-permute-done.1.far_mine = f32[18,128,128]{2,1,0:T(8,128)S(1)} collective-permute-done((f32[18,128,128]{2,1,0:T(8,128)}, f32[18,128,128]{2,1,0:T(8,128)S(1)}, u32[]{:S(2)}, u32[]{:S(2)}) %collective-permute-start.1) | collective-permute-done | bytes 1179680 | tf_op jit(solution)/shard_map/ppermute | solution.py:752
  165.4 0.0 copy-start
  165.4 1.1 collective-permute-start.2
  166.5 0.0 all-gather.16.cloned.1.call-update
  166.5 0.0 all-gather.14.cloned.1.call-done
  166.6 2.4 %collective-permute-done.2.far_other = f32[18,128,128]{2,1,0:T(8,128)S(1)} collective-permute-done((f32[18,128,128]{2,1,0:T(8,128)S(1)}, f32[18,128,128]{2,1,0:T(8,128)S(1)}, u32[]{:S(2)}, u32[]{:S(2)}) %collective-permute-start.2) | collective-permute-done | bytes 1179680 | tf_op jit(solution)/shard_map/ppermute | solution.py:752
  169.0 0.0 copy-start.1
  169.0 0.0 copy-done
  169.0 1.1 copy-done.1
  170.1 32.7 %chol_two.1 = (f32[8,1024,128]{2,1,0:T(8,128)}, f32[8,128,128]{2,1,0:T(8,128)}) custom-call(s32[5]{0:T(128)} %stack.23.ids, s32[8,2,16]{2,1,0:T(2,128)} %map_two.1, f32[16,512,128]{2,1,0:T(8,128)} %bitcast.14, f32[18,128,128]{2,1,0:T(8,128)} %get-tuple-element.37.near_mine, f32[18,128,128]{2,1,0:T(8,128)} %get-tuple-element.38.near_other, ...), custom_call_target="tpu_custom_call" | custom-call | flops 40000000000 | bytes 100000000 | tf_op jit(solution)/shard_map/chol_two/pallas_call | solution.py:737
  202.7 0.0 all-gather.16.cloned.1.call-done
  202.8 10.5 %tail.1 = (f32[512,128]{1,0:T(8,128)}, f32[256,128]{1,0:T(8,128)}) custom-call(s32[5]{0:T(128)} %stack.23.ids, s32[8,2,16]{2,1,0:T(2,128)} %map_two.1, f32[8,1024,128]{2,1,0:T(8,128)} %get-tuple-element.39.chol_in, f32[8,128,128]{2,1,0:T(8,128)} %get-tuple-element.40.inverse, f32[8,256,128]{2,1,0:T(8,128)} %bitcast.11, f32[4,256,128]{2,1,0:T(8,128)} %bitcast.10, ...), custom_call_target="tpu_custom_call" | custom-call | tf_op jit(solution)/shard_map/tail/pallas_call | solution.py:737
Async XLA Ops:
  7.2 61.0 %all-gather.10.cloned.1.call-start = ((), (), s32[]{:S(2)}) async-start(), calls=%async_computation | async-start | bytes 7798784 | tf_op jit(solution)/shard_map/all_gather | solution.py:778
  12.6 104.5 %all-gather.12.cloned.1.call-start = ((), (), s32[]{:S(2)}) async-start(), calls=%async_computation.1 | async-start | bytes 7241728 | tf_op jit(solution)/shard_map/all_gather | solution.py:799
  17.7 12.4 %collective-permute-start = (f32[256,128]{1,0:T(8,128)}, f32[256,128]{1,0:T(8,128)S(1)}, u32[]{:S(2)}, u32[]{:S(2)}) collective-permute-start(f32[256,128]{1,0:T(8,128)} %get-tuple-element.27), channel_id=1, source_target_pairs={{0,16},{16,0},{1,17},{17,1},{2,18},{18,2},{3,19},{19,3},{4,20},{20... | collective-permute-start | bytes 393224 | tf_op jit(solution)/shard_map/ppermute | solution.py:752
  68.2 98.4 %all-gather.14.cloned.1.call-start = ((), (), s32[]{:S(2)}) async-start(), calls=%async_computation.2 | async-start | bytes 4456448 | tf_op jit(solution)/shard_map/all_gather | solution.py:817
  68.9 133.9 %all-gather.16.cloned.1.call-start = ((), (), s32[]{:S(2)}) async-start(), calls=%async_computation.3 | async-start | bytes 1179648 | tf_op jit(solution)/shard_map/all_gather | solution.py:818
  137.8 27.6 %collective-permute-start.1 = (f32[18,128,128]{2,1,0:T(8,128)}, f32[18,128,128]{2,1,0:T(8,128)S(1)}, u32[]{:S(2)}, u32[]{:S(2)}) collective-permute-start(f32[18,128,128]{2,1,0:T(8,128)} %get-tuple-element.37.near_mine), channel_id=1, source_target_pairs={{0,16},{16,0},{1,17},{17,1},{2,18},{18,2},{3,19},{19,3},{4,20},{20... | collective-permute-start | bytes 3538952 | tf_op jit(solution)/shard_map/ppermute | solution.py:752
  165.4 3.6 %copy-start = (f32[18,128,128]{2,1,0:T(8,128)}, f32[18,128,128]{2,1,0:T(8,128)S(1)}, u32[]{:S(2)}) copy-start(f32[18,128,128]{2,1,0:T(8,128)S(1)} %collective-permute-done.1.far_mine) | copy-start | bytes 3538948
  165.4 3.5 %collective-permute-start.2 = (f32[18,128,128]{2,1,0:T(8,128)S(1)}, f32[18,128,128]{2,1,0:T(8,128)S(1)}, u32[]{:S(2)}, u32[]{:S(2)}) collective-permute-start(f32[18,128,128]{2,1,0:T(8,128)S(1)} %collective-permute-done.1.far_mine), channel_id=1, source_target_pairs={{0,8},{8,0},{1,9},{9,1},{2,10},{10,2},{3,11},{11,3},{4,12},{12,4},... | collective-permute-start | bytes 3538952 | tf_op jit(solution)/shard_map/ppermute | solution.py:752
  169.0 1.1 copy-start.1
Sparse Core Ops, SparseCore 0:
  12.7 55.3 all-gather.9
  70.0 47.0 all-gather.11
  119.5 40.7 all-gather.13
  166.7 31.6 all-gather.15

commit v2 on v1

--- a/solution.py
+++ b/solution.py
@@ -19,6 +19,9 @@
 LOWER_ROWS = 4 * BLK
 PARAMS = pltpu.CompilerParams(vmem_limit_bytes=58 * 1024 * 1024)
 LEAF = ("x", "yh", "yl", "core")
+MOST = 6
+SOON = 22
+LATE = 36 - SOON
 
 
 def shape(*dims):
@@ -174,6 +177,35 @@
     lax.fori_loop(0, NB, one_panel, 0)
 
 
+def factor_corner_again(work, chol, inverse):
+    def rows_of(block):
+        return pl.ds(pl.multiple_of(block * BLK, BLK), BLK)
+
+    def one_panel(step, carry):
+        lower, lower_inverse = factor_block(work[step, rows_of(step), :])
+        chol[step, rows_of(step), :] = lower
+        inverse[step] = lower_inverse
+
+        def one_block(i, carry):
+            chol[step, rows_of(i), :] = dot_split(work[step, rows_of(i), :], inverse[step])
+            return carry
+
+        def one_col(k, carry):
+            def one_row(i, carry):
+                work[k, rows_of(i), :] = work[k, rows_of(i), :] - dot_split(
+                    chol[step, rows_of(i), :], chol[step, rows_of(k), :]
+                )
+                return carry
+
+            return lax.fori_loop(k, NB, one_row, carry)
+
+        lax.fori_loop(step + 1, NB, one_block, 0)
+        return lax.fori_loop(step + 1, NB, one_col, carry)
+
+    chol[...] = jnp.zeros_like(chol)
+    lax.fori_loop(0, NB, one_panel, 0)
+
+
 def solve_rows(right_side, chol, inverse, solved, solved_high, solved_low):
     for p in range(0, NB, 2):
         value = right_side(p)
@@ -326,37 +358,55 @@
     lax.fori_loop(0, 72, one, 0)
 
 
-def add_packed_separators(block_map, front, children, work, evens):
-    def one_child(child, carry):
-        count = jnp.int32(0)
+def ordered(block_map, front, child, order, place):
+    count = jnp.int32(0)
+    for parity in range(2):
         for i in range(NB):
-            evens[count] = i
-            count = count + 1 - block_map[front, child, i] % 2
-
-        def one_col(b, carry):
-            k = evens[b]
-            col = block_map[front, child, k] // 2
-
-            def one_row(a, carry):
-                i = evens[a]
-                row = block_map[front, child, i] // 2
-                index = packed_index(i, k)
+            hit = block_map[front, child, i] % 2 == parity
+
+            @pl.when(hit)
+            def _(count=count, i=i):
+                order[child, count] = i
+                place[child, i] = count
+
+            count = count + jnp.where(hit, 1, 0)
+        if parity == 0:
+            separators = count
+    return separators
+
+
+def number_of(a, b):
+    return a * (a + 1) // 2 + b
+
+
+def block_number(place, child, i, k):
+    a, b = place[child, i], place[child, k]
+    return number_of(jnp.maximum(a, b), jnp.minimum(a, b))
+
+
+def add_ordered_separators(block_map, front, children, work, order, counts):
+    for child in range(2):
+
+        def one_place(a, carry):
+            def other_place(b, carry):
+                i, k = order[child, a], order[child, b]
+                row = block_map[front, child, jnp.maximum(i, k)] // 2
+                col = block_map[front, child, jnp.minimum(i, k)] // 2
+                number = number_of(a, b)
 
                 @pl.when(row >= col)
                 def _():
-                    add_at(work, col, row, children[child, index])
+                    add_at(work, col, row, children[child, number])
 
                 @pl.when(row < col)
                 def _():
-                    add_at(work, row, col, children[child, index].T)
+                    add_at(work, row, col, children[child, number].T)
 
                 return carry
 
-            return lax.fori_loop(b, count, one_row, carry)
-
-        return lax.fori_loop(0, count, one_col, carry)
-
-    lax.fori_loop(0, 2, one_child, 0)
+            return lax.fori_loop(0, a + 1, other_place, carry)
+
+        lax.fori_loop(0, counts[child], one_place, 0)
 
 
 def add_at(ref, lead, block_row, block):
@@ -494,6 +544,7 @@
 
 def rest_kernel(
     ids,
+    block_map,
     chol_in,
     inverse_in,
     lower_in,
@@ -502,6 +553,7 @@
     factor,
     mine,
     other,
+    late,
     chol,
     inverse,
     lower,
@@ -511,9 +563,12 @@
     solved_low,
     trail,
     trail_add,
+    staged,
+    order,
+    place,
     sems,
 ):
-    side, z = ids[1], ids[2]
+    side, z, child = ids[1], ids[2], ids[4] // 2
     half = NB // 2 * BLK
     used = []
 
@@ -547,6 +602,7 @@
                 )
             )
             start += rows
+    ordered(block_map, ids[3], child, order, place)
     for copy in first:
         copy.wait()
 
@@ -566,14 +622,18 @@
         for w in range(2):
             for i in range(p + w, NB):
                 index = packed_index(i, p + w)
-                trail[index] = (
+                number = block_number(place, child, i, p + w)
+                half_id = jnp.where(number < SOON // 2, 0, 1)
+                soon = (half_id + side) % 2 * (SOON // 2) + number - half_id * (SOON // 2)
+                staged[jnp.where(number < SOON, soon, number)] = (
                     trail[index]
                     + trail_add[index]
                     - update[(i - p) * BLK : (i - p + 1) * BLK, w * BLK : (w + 1) * BLK]
                 )
     outs = [
-        pltpu.make_async_copy(trail.at[pl.ds(18 * side, 18)], mine, sems.at[0]),
-        pltpu.make_async_copy(trail.at[pl.ds(18 * (1 - side), 18)], other, sems.at[1]),
+        pltpu.make_async_copy(staged.at[: SOON // 2], mine, sems.at[0]),
+        pltpu.make_async_copy(staged.at[SOON // 2 : SOON], other, sems.at[1]),
+        pltpu.make_async_copy(staged.at[SOON:], late, sems.at[2]),
     ]
     for copy in outs:
         copy.start()
@@ -587,8 +647,9 @@
 
 def fetch_children(side, mine, refs, children, sems):
     near_mine, near_other, far_mine, far_other = refs
+    half = SOON // 2
     copies = []
-    for n, (ref, child, half) in enumerate(
+    for n, (ref, child, half_id) in enumerate(
         (
             (near_mine, mine, side),
             (near_other, mine, 1 - side),
@@ -596,8 +657,25 @@
             (far_other, 1 - mine, 1 - side),
         )
     ):
-        copies.append(pltpu.make_async_copy(ref, children.at[child, pl.ds(18 * half, 18)], sems.at[n]))
+        target = children.at[child, pl.ds(half * half_id, half)]
+        copies.append(pltpu.make_async_copy(ref, target, sems.at[n]))
         copies[-1].start()
+    return copies
+
+
+def corner_copies(side_of, gathered, work, sems):
+    copies = []
+    for core in range(2):
+        for n, y in ((0, side_of), (1, 1 - side_of)):
+            start = pl.multiple_of(2 * (2 * y + core) * BLK, BLK)
+            copies.append(
+                pltpu.make_async_copy(
+                    gathered.at[core * NB : (core + 1) * NB, 2 * n * BLK : 2 * (n + 1) * BLK, :],
+                    work.at[:, pl.ds(start, 2 * BLK), :],
+                    sems.at[2 * core + n],
+                )
+            )
+            copies[-1].start()
     return copies
 
 
@@ -613,35 +691,31 @@
     inverse,
     work,
     children,
-    evens,
+    order,
+    place,
     sems,
+    corner_sems,
 ):
     side, front, sub = ids[1], ids[3], ids[4]
     copies = fetch_children(
         side, sub // 2, (near_mine, near_other, far_mine, far_other), children, sems
     )
-    for core in range(2):
-        for n, y in ((0, sub // 2), (1, 1 - sub // 2)):
-            start = pl.multiple_of(2 * (2 * y + core) * BLK, BLK)
-            copies.append(
-                pltpu.make_async_copy(
-                    gathered.at[core * NB : (core + 1) * NB, 2 * n * BLK : 2 * (n + 1) * BLK, :],
-                    work.at[:, pl.ds(start, 2 * BLK), :],
-                    sems.at[4 + 2 * core + n],
-                )
-            )
-            copies[-1].start()
+    copies += corner_copies(sub // 2, gathered, work, corner_sems)
+    counts = [
+        jnp.minimum(ordered(block_map, front, child, order, place), MOST) for child in range(2)
+    ]
     for copy in copies:
         copy.wait()
-    add_packed_separators(block_map, front, children, work, evens)
+    add_ordered_separators(block_map, front, children, work, order, counts)
     factor_corner(work, chol, inverse)
 
 
 def tail_kernel(
     ids,
     map_two,
+    gathered,
     chol_in,
-    inverse,
+    inverse_in,
     lower_near,
     rows_all,
     tail,
@@ -649,9 +723,13 @@
     near_other,
     far_mine,
     far_other,
+    near_late,
+    far_late,
     factor,
     schur,
     chol,
+    inverse,
+    work,
     children,
     lower,
     solved,
@@ -659,15 +737,28 @@
     solved_low,
     trail,
     slots,
+    order,
+    place,
     sems,
+    corner_sems,
 ):
     side, z, front, sub = ids[1], ids[2], ids[3], ids[4]
     mine = sub // 2
     copies = fetch_children(
         side, mine, (near_mine, near_other, far_mine, far_other), children, sems
     )
-    chol_copy = pltpu.make_async_copy(chol_in, chol, sems.at[4])
-    chol_copy.start()
+    for n, (ref, child) in enumerate(((near_late, mine), (far_late, 1 - mine))):
+        copies.append(
+            pltpu.make_async_copy(ref, children.at[child, pl.ds(SOON, LATE)], sems.at[4 + n])
+        )
+        copies[-1].start()
+    factors = [
+        pltpu.make_async_copy(chol_in, chol, sems.at[6]),
+        pltpu.make_async_copy(inverse_in, inverse, sems.at[7]),
+    ]
+    for copy in factors:
+        copy.start()
+    counts = [ordered(map_two, front, child, order, place) for child in range(2)]
     place_of(map_two, front, 0, slots)
     place_of(map_two, front, 1, slots)
     lower[:, : 2 * BLK, :] = lower_near[...]
@@ -685,7 +776,7 @@
 
             def one_block(k, carry):
                 col = map_two[front, child, k]
-                index = packed_index(jnp.maximum(i, k), jnp.minimum(i, k))
+                index = block_number(place, child, i, k)
 
                 @pl.when((col % 2 == 0) & (i > k))
                 def _():
@@ -702,7 +793,7 @@
         for slot in range(2):
             i = slots[child, 2 * wanted[slot] + 1]
             both = (i >= 0) & (k >= 0)
-            index = jnp.where(both, packed_index(jnp.maximum(i, k), jnp.minimum(i, k)), 0)
+            index = block_number(place, child, jnp.maximum(i, 0), jnp.maximum(k, 0))
 
             @pl.when(both & (i >= k))
             def _():
@@ -715,7 +806,16 @@
         return carry
 
     lax.fori_loop(0, 2, one_child, 0)
-    chol_copy.wait()
+    for copy in factors:
+        copy.wait()
+
+    @pl.when(jnp.maximum(counts[0], counts[1]) > MOST)
+    def _():
+        for copy in corner_copies(mine, gathered, work, corner_sems):
+            copy.wait()
+        add_ordered_separators(map_two, front, children, work, order, counts)
+        factor_corner_again(work, chol, inverse)
+
     solve_rows(lambda p: pair(lower, p), chol, inverse, solved, solved_high, solved_low)
     high = jnp.concatenate([solved_high[k] for k in range(NB)], 1)
     low = jnp.concatenate([solved_low[k] for k in range(NB)], 1)
@@ -816,23 +916,31 @@
     lower_two, _ = lax.optimization_barrier((lower_two, gathered))
     gathered_two = lax.all_gather(corner_two, ("core", "front"), axis=0, tiled=False)
     lower_near = lax.all_gather(lower_two, "front", axis=0, tiled=False)
-    factor_one, near_mine, near_other = call(
+    places = pltpu.SMEM((2, NB), jnp.int32)
+    factor_one, near_mine, near_other, near_late = call(
         rest_kernel,
         "rest",
-        [shape(NB * BLK, BLK), shape(18, *block), shape(18, *block)],
-        [SMEM] + [ANY] * 5,
-        (ids, chol, inverse, lower_add, trail_add, merged_all),
+        [
+            shape(NB * BLK, BLK),
+            shape(SOON // 2, *block),
+            shape(SOON // 2, *block),
+            shape(LATE, *block),
+        ],
+        [SMEM, SMEM] + [ANY] * 5,
+        (ids, parent_map_two, chol, inverse, lower_add, trail_add, merged_all),
         [pltpu.VMEM(panel, F32), pltpu.VMEM((NB, *block), F32)]
         + [pltpu.VMEM(panel, F32)] * 3
         + [pltpu.VMEM(panel, BF16)] * 2
-        + [pltpu.VMEM((36, *block), F32)] * 2
-        + [pltpu.SemaphoreType.DMA((64,))],
+        + [pltpu.VMEM((36, *block), F32)] * 3
+        + [places, places, pltpu.SemaphoreType.DMA((64,))],
         flops=15_000_000_000,
-        out_specs=[VMEM, ANY, ANY],
+        out_specs=[VMEM, ANY, ANY, ANY],
     )
     far_mine = swap(near_mine, "yl")
     far_other = swap(far_mine, "core")
     packed = (near_mine, near_other, far_mine, far_other)
+    given_late, _ = lax.optimization_barrier((near_late, far_mine))
+    far_late = swap(given_late, "yl")
     children = pltpu.VMEM((2, 36, *block), F32)
     chol, inverse = call(
         chol_two_kernel,
@@ -843,8 +951,10 @@
         [
             pltpu.VMEM(panel, F32),
             children,
-            pltpu.SMEM((NB + 1,), jnp.int32),
-            pltpu.SemaphoreType.DMA((8,)),
+            places,
+            places,
+            pltpu.SemaphoreType.DMA((4,)),
+            pltpu.SemaphoreType.DMA((4,)),
         ],
         flops=40_000_000_000,
     )
@@ -853,9 +963,23 @@
         tail_kernel,
         "tail",
         [shape(4 * BLK, BLK), shape(2 * BLK, BLK)],
-        [SMEM, SMEM, ANY] + [VMEM] * 4 + [ANY] * 4,
-        (ids, parent_map_two, chol, inverse, lower_near, rows_all, tail_two, *packed),
+        [SMEM, SMEM, ANY, ANY, ANY] + [VMEM] * 3 + [ANY] * 6,
+        (
+            ids,
+            parent_map_two,
+            gathered_two,
+            chol,
+            inverse,
+            lower_near,
+            rows_all,
+            tail_two,
+            *packed,
+            near_late,
+            far_late,
+        ),
         [
+            pltpu.VMEM(panel, F32),
+            pltpu.VMEM((NB, *block), F32),
             pltpu.VMEM(panel, F32),
             children,
             pltpu.VMEM(rows, F32),
@@ -864,7 +988,10 @@
             pltpu.VMEM(rows, BF16),
             pltpu.VMEM((2, *block), F32),
             pltpu.SMEM((2, FB), jnp.int32),
-            pltpu.SemaphoreType.DMA((5,)),
+            places,
+            places,
+            pltpu.SemaphoreType.DMA((8,)),
+            pltpu.SemaphoreType.DMA((4,)),
         ],
     )
     return factor_one, factor_two, schur_two

time: 221 us -> 218 us (0.986)
  the two profiles are of different devices: /device:TPU:1 before, /device:TPU:16 now
where the time goes in v2:
time: 218 us; the launch traced here: 217 us
  Pallas kernels  116 us (53%)
  waiting for transfers between devices  70.5 us (32%)
  between operations  13.8 us (6%)
  blocking collectives  8.28 us (4%)
  starting transfers between devices  4.02 us (2%)
  local copies, waits for them, and re-layouts  2.47 us (1%)
    pallas_call x6, Pallas kernels, call(): pl.pallas_call(kernel, name=name, out_shape=outs, in_specs=specs, out_spe...  116 us
    all_gather x1, waiting for transfers between devices, per_device(): gathered = lax.all_gather(sent, ('core', 'front'), axis=0, tiled=False)  37.9 us
    ppermute x4, waiting for transfers between devices, swap(): return lax.ppermute(value, axis, [(0, 1), (1, 0)])  17.3 us
    all_gather x1, blocking collectives, per_device(): rows_all = lax.all_gather(row_two, ('yl', 'core'), axis=0, tiled=False)  8.28 us
    all_gather x1, waiting for transfers between devices, per_device(): merged_all = lax.all_gather(merged, ('core', 'front'), axis=0, tiled=False)  7.47 us
    all_gather x1, waiting for transfers between devices, per_device(): lower_near = lax.all_gather(lower_two, 'front', axis=0, tiled=False)  4.92 us
  transfers between devices with their start and end apart: 8, of which 5 were waited for; matrix products, arithmetic and copies ran while one was open for 1% of the time, Pallas kernels for 46%

profile of v2, /device:TPU:16, one launch (start us, length us, event | category | flops | bytes accessed | tf_op | source)
XLA Modules:
  0.0 217.1 jit_solution(15445957832113229922)
XLA Ops:
  7.2 0.0 all-gather.10.cloned.1.call-start
  7.2 0.7 stack.23.ids
  7.9 4.7 %pack.1 = f32[896,128]{1,0:T(8,128)} custom-call(s32[5]{0:T(128)} %stack.23.ids, s32[16,16,16]{2,1,0:T(8,128)} %pattern_one.3, f32[1024,128]{1,0:T(8,128)} %child.1, f32[1024,256]{1,0:T(8,128)} %initial_one.1), custom_call_target="tpu_custom_call" | custom-call | tf_op jit(solution)/shard_map/pack/pallas_call | solution.py:837
  12.6 0.0 all-gather.10.cloned.1.call-update
  12.6 0.0 all-gather.12.cloned.1.call-start
  12.7 5.0 %mask.1 = (f32[832,128]{1,0:T(8,128)}, f32[256,128]{1,0:T(8,128)}, f32[256,128]{1,0:T(8,128)}, f32[256,128]{1,0:T(8,128)}, f32[2,128,128]{2,1,0:T(8,128)}) custom-call(s32[5]{0:T(128)} %stack.23.ids, s32[16,16,16]{2,1,0:T(8,128)} %pattern_one.3, s32[8,16,16]{2,1,0:T(8,128)} %pattern_two.1, f32[1024,256]{1,0:T(8,128)} %initial_one.1, f32[512,256]{1,0:T(8,128)} %initial_two.1), custom_call_target="tpu_custom_call" | custom-call | tf_op jit(solution)/shard_map/mask/pallas_call | solution.py:837
  17.6 1.3 collective-permute-start
  18.9 8.3 %all-gather.1 = f32[1024,128]{1,0:T(8,128)} all-gather(f32[256,128]{1,0:T(8,128)} %get-tuple-element.30), channel_id=3, replica_groups=mesh['x'=4,'yh'=2,'yl'=2,'core'=2,'front'=8] {'yl','core'}, dimensions={0}, use_global_device_ids=true | all-gather | bytes 655360 | tf_op jit(solution)/shard_map/all_gather | solution.py:895
  27.2 0.0 collective-permute-done
  27.2 1.6 pad_maximum_fusion
  28.8 37.9 %all-gather.10.cloned.1.call-done = f32[14336,128]{1,0:T(8,128)} async-done(((f32[896,128]{1,0:T(8,128)}), f32[14336,128]{1,0:T(8,128)}) %all-gather.10.cloned.1.call-update) | async-done | bytes 7340048 | tf_op jit(solution)/shard_map/all_gather | solution.py:878
  66.7 0.0 all-gather.12.cloned.1.call-update
  66.7 0.0 all-gather.14.cloned.1.call-start
  66.8 0.7 all-gather.14.cloned.1.call-update
  67.5 0.0 all-gather.16.cloned.1.call-start
  67.5 40.7 %chol.1 = (f32[8,1024,128]{2,1,0:T(8,128)}, f32[8,128,128]{2,1,0:T(8,128)}, f32[8,1024,128]{2,1,0:T(8,128)}, f32[36,128,128]{2,1,0:T(8,128)}) custom-call(s32[5]{0:T(128)} %stack.23.ids, s32[16,2,16]{2,1,0:T(2,128)} %block_map.3, f32[16,896,128]{2,1,0:T(8,128)} %bitcast.14), custom_call_target="tpu_custom_call" | custom-call | flops 40000000000 | bytes 100000000 | tf_op jit(solution)/shard_map/chol/pallas_call | solution.py:837
  108.2 7.5 %all-gather.12.cloned.1.call-done = f32[13312,128]{1,0:T(8,128)} async-done(((f32[832,128]{1,0:T(8,128)}), f32[13312,128]{1,0:T(8,128)}) %all-gather.12.cloned.1.call-update) | async-done | bytes 6815760 | tf_op jit(solution)/shard_map/all_gather | solution.py:899
  115.7 21.0 %rest.1 = (f32[1024,128]{1,0:T(8,128)}, f32[11,128,128]{2,1,0:T(8,128)}, f32[11,128,128]{2,1,0:T(8,128)}, f32[14,128,128]{2,1,0:T(8,128)}) custom-call(s32[5]{0:T(128)} %stack.23.ids, s32[8,2,16]{2,1,0:T(2,128)} %map_two.1, f32[8,1024,128]{2,1,0:T(8,128)} %get-tuple-element.32.chol_in, f32[8,128,128]{2,1,0:T(8,128)} %get-tuple-element.33.inverse_in, ...), custom_call_target="tpu_custom_call" | custom-call | flops 15000000512 | bytes 37500000 | tf_op jit(solution)/shard_map/rest/pallas_call | solution.py:837
  136.7 1.3 collective-permute-start.1
  137.9 17.3 %collective-permute-done.1.far_mine = f32[11,128,128]{2,1,0:T(8,128)S(1)} collective-permute-done((f32[11,128,128]{2,1,0:T(8,128)}, f32[11,128,128]{2,1,0:T(8,128)S(1)}, u32[]{:S(2)}, u32[]{:S(2)}) %collective-permute-start.1) | collective-permute-done | bytes 720928 | tf_op jit(solution)/shard_map/ppermute | solution.py:852
  155.3 0.0 copy-start.1
  155.3 0.0 collective-permute-start.2
  155.3 0.0 all-gather.16.cloned.1.call-update
  155.3 1.3 collective-permute-start.3
  156.6 2.2 %all-gather.14.cloned.1.call-done = f32[8192,128]{1,0:T(8,128)} async-done(((f32[512,128]{1,0:T(8,128)}), f32[8192,128]{1,0:T(8,128)}) %all-gather.14.cloned.1.call-update) | async-done | bytes 4194320 | tf_op jit(solution)/shard_map/all_gather | solution.py:917
  158.8 0.0 collective-permute-done.2.far_other
  158.8 0.0 copy-start.2
  158.8 0.0 copy-done.1
  158.8 0.9 copy-done.2
  159.7 32.9 %chol_two.1 = (f32[8,1024,128]{2,1,0:T(8,128)}, f32[8,128,128]{2,1,0:T(8,128)}) custom-call(s32[5]{0:T(128)} %stack.23.ids, s32[8,2,16]{2,1,0:T(2,128)} %map_two.1, f32[16,512,128]{2,1,0:T(8,128)} %bitcast.10, f32[11,128,128]{2,1,0:T(8,128)} %get-tuple-element.39.near_mine, f32[11,128,128]{2,1,0:T(8,128)} %get-tuple-element.40.near_other, ...), custom_call_target="tpu_custom_call" | custom-call | flops 40000000000 | bytes 100000000 | tf_op jit(solution)/shard_map/chol_two/pallas_call | solution.py:837
  192.6 4.9 %all-gather.16.cloned.1.call-done = f32[2048,128]{1,0:T(8,128)} async-done(((f32[256,128]{1,0:T(8,128)}), f32[2048,128]{1,0:T(8,128)}) %all-gather.16.cloned.1.call-update) | async-done | bytes 1048592 | tf_op jit(solution)/shard_map/all_gather | solution.py:918
  197.5 0.0 collective-permute-done.3.far_late
  197.5 0.0 copy-start
  197.5 0.9 copy-done
  198.4 12.1 %tail.1 = (f32[512,128]{1,0:T(8,128)}, f32[256,128]{1,0:T(8,128)}) custom-call(s32[5]{0:T(128)} %stack.23.ids, s32[8,2,16]{2,1,0:T(2,128)} %map_two.1, f32[16,512,128]{2,1,0:T(8,128)} %bitcast.11, f32[8,1024,128]{2,1,0:T(8,128)} %get-tuple-element.41.chol_in, f32[8,128,128]{2,1,0:T(8,128)} %get-tuple-element.42.inverse_in, f32[8,256,128]{2,1,0:T(8,128)} %bitcast.13, ...), custom_call_target="tpu_custom_call" | custom-call | tf_op jit(solution)/shard_map/tail/pallas_call | solution.py:837
Async XLA Ops:
  7.2 59.5 %all-gather.10.cloned.1.call-start = ((), (), s32[]{:S(2)}) async-start(), calls=%async_computation | async-start | bytes 7798784 | tf_op jit(solution)/shard_map/all_gather | solution.py:878
  12.6 103.0 %all-gather.12.cloned.1.call-start = ((), (), s32[]{:S(2)}) async-start(), calls=%async_computation.1 | async-start | bytes 7241728 | tf_op jit(solution)/shard_map/all_gather | solution.py:899
  17.6 9.6 %collective-permute-start = (f32[256,128]{1,0:T(8,128)}, f32[256,128]{1,0:T(8,128)S(1)}, u32[]{:S(2)}, u32[]{:S(2)}) collective-permute-start(f32[256,128]{1,0:T(8,128)} %get-tuple-element.29), channel_id=1, source_target_pairs={{0,16},{16,0},{1,17},{17,1},{2,18},{18,2},{3,19},{19,3},{4,20},{20... | collective-permute-start | bytes 393224 | tf_op jit(solution)/shard_map/ppermute | solution.py:852
  66.7 92.1 %all-gather.14.cloned.1.call-start = ((), (), s32[]{:S(2)}) async-start(), calls=%async_computation.2 | async-start | bytes 4456448 | tf_op jit(solution)/shard_map/all_gather | solution.py:917
  67.5 130.0 %all-gather.16.cloned.1.call-start = ((), (), s32[]{:S(2)}) async-start(), calls=%async_computation.3 | async-start | bytes 1179648 | tf_op jit(solution)/shard_map/all_gather | solution.py:918
  136.7 18.6 %collective-permute-start.1 = (f32[11,128,128]{2,1,0:T(8,128)}, f32[11,128,128]{2,1,0:T(8,128)S(1)}, u32[]{:S(2)}, u32[]{:S(2)}) collective-permute-start(f32[11,128,128]{2,1,0:T(8,128)} %get-tuple-element.39.near_mine), channel_id=1, source_target_pairs={{0,16},{16,0},{1,17},{17,1},{2,18},{18,2},{3,19},{19,3},{4,20},{20... | collective-permute-start | bytes 2162696 | tf_op jit(solution)/shard_map/ppermute | solution.py:852
  155.3 3.6 %copy-start.1 = (f32[11,128,128]{2,1,0:T(8,128)}, f32[11,128,128]{2,1,0:T(8,128)S(1)}, u32[]{:S(2)}) copy-start(f32[11,128,128]{2,1,0:T(8,128)S(1)} %collective-permute-done.1.far_mine) | copy-start | bytes 2162692
  155.3 3.6 %collective-permute-start.2 = (f32[11,128,128]{2,1,0:T(8,128)S(1)}, f32[11,128,128]{2,1,0:T(8,128)S(1)}, u32[]{:S(2)}, u32[]{:S(2)}) collective-permute-start(f32[11,128,128]{2,1,0:T(8,128)S(1)} %collective-permute-done.1.far_mine), channel_id=1, source_target_pairs={{0,8},{8,0},{1,9},{9,1},{2,10},{10,2},{3,11},{11,3},{4,12},{12,4},... | collective-permute-start | bytes 2162696 | tf_op jit(solution)/shard_map/ppermute | solution.py:852
  155.3 42.2 %collective-permute-start.3 = (f32[14,128,128]{2,1,0:T(8,128)}, f32[14,128,128]{2,1,0:T(8,128)S(1)}, u32[]{:S(2)}, u32[]{:S(2)}) collective-permute-start(f32[14,128,128]{2,1,0:T(8,128)} %get-tuple-element.48.near_late), channel_id=1, source_target_pairs={{0,16},{16,0},{1,17},{17,1},{2,18},{18,2},{3,19},{19,3},{4,20},{20... | collective-permute-start | bytes 2752520 | tf_op jit(solution)/shard_map/ppermute | solution.py:852
  158.8 0.9 copy-start.2
  197.5 0.9 copy-start
Sparse Core Ops, SparseCore 0:
  12.7 53.9 all-gather.9
  68.5 47.0 all-gather.11
  118.1 40.7 all-gather.13
  160.5 37.0 all-gather.15

commit v3 on v2

--- a/solution.py
+++ b/solution.py
@@ -52,13 +52,16 @@
         if t + 1 < last:
             following = lane_columns(rows[t + 1], t + 1)
         scale, weight = [], {}
+        ahead = across(head[0][0:1])
         for b in range(8):
-            pivot = across(head[b][b : b + 1])
+            pivot = ahead
             scale.append(lax.rsqrt(pivot))
             diag = jnp.where(lane == 8 * t + b, pivot * scale[b], diag)
             low = head[b] * scale[b]
             for a in range(b + 1, 8):
-                weight[a, b] = across(low[a : a + 1])
+                weight[a, b] = across(head[b][a : a + 1]) * scale[b]
+                if a == b + 1:
+                    ahead = across(head[a][a : a + 1]) - weight[a, b] * weight[a, b]
                 head[a] = head[a] - low * weight[a, b]
         inside = (lane >= 8 * t) & (lane < 8 * t + 8)
         pivots = []
@@ -451,15 +454,26 @@
     return jnp.where(keep, initial[local * BLK : (local + 1) * BLK, :], 0.0)
 
 
-def pack_kernel(ids, pattern_one, child, initial, merged, columns, tile, sem):
+def pack_kernel(ids, pattern_one, child_in, initial, sent, child, corner, trail, sems):
     front_one, side, z = ids[0], ids[1], ids[2]
-    copy = pltpu.make_async_copy(initial.at[:, :BLK], columns, sem)
-    copy.start()
-    send_child(child, z, merged.at[:CHILD_ROWS, :])
-    copy.wait()
-    for r in range(4):
-        tile[r] = masked_tile(columns, pattern_one, front_one, NB * side + 2 * r, 2 * r, 2 * z)
-    send_blocks(tile, side, z, merged.at[CHILD_ROWS:, :])
+    copies = [pltpu.make_async_copy(child_in, child, sems.at[NB])]
+    for r in range(NB):
+        w = r % 2
+        source = initial.at[r * BLK : (r + 1) * BLK, w * BLK : (w + 1) * BLK]
+        target = (trail if w else corner).at[r // 2]
+        copies.append(pltpu.make_async_copy(source, target, sems.at[r]))
+    for copy in copies:
+        copy.start()
+    copies[0].wait()
+    send_child(child, z, sent.at[:CHILD_ROWS, :])
+    for copy in copies[1:]:
+        copy.wait()
+    for r in range(NB):
+        tile = trail if r % 2 else corner
+        keep = kept(pattern_one, front_one, NB * side + r, 2 * z + r % 2)
+        tile[r // 2] = jnp.where(keep, tile[r // 2], 0.0)
+    send_blocks(corner, side, z, sent.at[CHILD_ROWS : CHILD_ROWS + CORNER_ROWS, :])
+    send_blocks(trail, side, z, sent.at[CHILD_ROWS + CORNER_ROWS :, :])
 
 
 def mask_kernel(
@@ -473,17 +487,14 @@
     lower_two,
     row_two,
     tail_two,
-    tile,
 ):
     front_one, side, z, front_two, sub = ids[0], ids[1], ids[2], ids[3], ids[4]
-    first, second = initial_one.at[:, :BLK], initial_one.at[:, BLK:]
+    first = initial_one.at[:, :BLK]
     for r in range(4):
         row = NB * side + 2 * r + 1
         merged[r * BLK : (r + 1) * BLK, :] = masked_tile(
             first, pattern_one, front_one, row, 2 * r + 1, 2 * z
         )
-        tile[r] = masked_tile(second, pattern_one, front_one, row, 2 * r + 1, 2 * z + 1)
-    send_blocks(tile, side, z, merged.at[LOWER_ROWS:, :])
     for r in range(4):
         for w in range(2):
             columns = initial_two.at[:, w * BLK : (w + 1) * BLK]
@@ -514,20 +525,21 @@
     front = ids[0]
     copies = child_copies(gathered, children, sems)
     for (row, col), parts in static_blocks().items():
-        start = row * BLK
+        start = 0
         for piece, at, rows in parts:
-            copies.append(
-                pltpu.make_async_copy(
-                    gathered.at[piece, CHILD_ROWS + at : CHILD_ROWS + at + rows, :],
-                    work.at[col, start : start + rows, :],
-                    sems.at[len(copies)],
-                )
-            )
+            for base, target in (
+                (CHILD_ROWS, work.at[col, row * BLK + start : row * BLK + start + rows, :]),
+                (
+                    CHILD_ROWS + CORNER_ROWS,
+                    trail.at[packed_index(row, col), start : start + rows, :],
+                ),
+            ):
+                source = gathered.at[piece, base + at : base + at + rows, :]
+                copies.append(pltpu.make_async_copy(source, target, sems.at[len(copies)]))
             start += rows
     for copy in copies:
         copy.start()
     lower[...] = jnp.zeros_like(lower)
-    trail[...] = jnp.zeros_like(trail)
     for copy in copies:
         copy.wait()
     each_gathered(block_map, front, children, contributions_into(work, lower, trail))
@@ -562,7 +574,6 @@
     solved_high,
     solved_low,
     trail,
-    trail_add,
     staged,
     order,
     place,
@@ -585,23 +596,13 @@
         for core in range(2):
             columns[p].append(
                 fetch(
-                    merged.at[core * NB + p : core * NB + p + 2, :LOWER_ROWS, :],
+                    merged.at[core * NB + p : core * NB + p + 2],
                     lower.at[p : p + 2, core * half : (core + 1) * half, :],
                 )
             )
         if p == 0:
             first.append(fetch(chol_in, chol))
-    last = [fetch(trail_in, trail_add)]
-    for (row, col), parts in static_blocks().items():
-        start = 0
-        for piece, at, rows in parts:
-            last.append(
-                fetch(
-                    merged.at[piece, LOWER_ROWS + at : LOWER_ROWS + at + rows, :],
-                    trail.at[packed_index(row, col), start : start + rows, :],
-                )
-            )
-            start += rows
+    last = fetch(trail_in, trail)
     ordered(block_map, ids[3], child, order, place)
     for copy in first:
         copy.wait()
@@ -612,8 +613,7 @@
         return pair(lower, p) + pair(lower_add, p)
 
     solve_rows(right_side, chol, inverse, solved, solved_high, solved_low)
-    for copy in last:
-        copy.wait()
+    last.wait()
     for p in range(0, NB, 2):
         high = jnp.concatenate([solved_high[k, p * BLK :, :] for k in range(NB)], 1)
         low = jnp.concatenate([solved_low[k, p * BLK :, :] for k in range(NB)], 1)
@@ -627,7 +627,6 @@
                 soon = (half_id + side) % 2 * (SOON // 2) + number - half_id * (SOON // 2)
                 staged[jnp.where(number < SOON, soon, number)] = (
                     trail[index]
-                    + trail_add[index]
                     - update[(i - p) * BLK : (i - p + 1) * BLK, w * BLK : (w + 1) * BLK]
                 )
     outs = [
@@ -716,7 +715,6 @@
     gathered,
     chol_in,
     inverse_in,
-    lower_near,
     rows_all,
     tail,
     near_mine,
@@ -752,6 +750,14 @@
             pltpu.make_async_copy(ref, children.at[child, pl.ds(SOON, LATE)], sems.at[4 + n])
         )
         copies[-1].start()
+    copies.append(
+        pltpu.make_async_copy(
+            gathered.at[pl.ds(side * NB, NB), 4 * BLK :, :],
+            lower.at[:, : 2 * BLK, :],
+            sems.at[8],
+        )
+    )
+    copies[-1].start()
     factors = [
         pltpu.make_async_copy(chol_in, chol, sems.at[6]),
         pltpu.make_async_copy(inverse_in, inverse, sems.at[7]),
@@ -761,7 +767,6 @@
     counts = [ordered(map_two, front, child, order, place) for child in range(2)]
     place_of(map_two, front, 0, slots)
     place_of(map_two, front, 1, slots)
-    lower[:, : 2 * BLK, :] = lower_near[...]
     for s in range(4):
         for b in range(2):
             lower[2 * s + b, 2 * BLK :, :] = rows_all[s, b * BLK : (b + 1) * BLK, :]
@@ -870,10 +875,15 @@
     (sent,) = call(
         pack_kernel,
         "pack",
-        [shape(CHILD_ROWS + CORNER_ROWS, BLK)],
-        [SMEM, SMEM, VMEM, ANY],
+        [shape(CHILD_ROWS + 2 * CORNER_ROWS, BLK)],
+        [SMEM, SMEM, ANY, ANY],
         (ids, pattern_one, child_updates, initial_one),
-        [pltpu.VMEM((NB * BLK, BLK), F32), pltpu.VMEM((4, *block), F32), pltpu.SemaphoreType.DMA],
+        [
+            pltpu.VMEM((NB * BLK, BLK), F32),
+            pltpu.VMEM((4, *block), F32),
+            pltpu.VMEM((4, *block), F32),
+            pltpu.SemaphoreType.DMA((NB + 1,)),
+        ],
     )
     gathered = lax.all_gather(sent, ("core", "front"), axis=0, tiled=False)
     ids_mask, _ = lax.optimization_barrier((ids, sent))
@@ -881,7 +891,7 @@
         mask_kernel,
         "mask",
         [
-            shape(LOWER_ROWS + CORNER_ROWS, BLK),
+            shape(LOWER_ROWS, BLK),
             shape(2 * BLK, BLK),
             shape(2 * BLK, BLK),
             shape(2 * BLK, BLK),
@@ -889,9 +899,8 @@
         ],
         [SMEM, SMEM, SMEM, VMEM, VMEM],
         (ids_mask, pattern_one, pattern_two, initial_one, initial_two),
-        [pltpu.VMEM((4, *block), F32)],
-    )
-    corner_two = jnp.concatenate([corner_two, swap(corner_two, "yl")], 0)
+    )
+    corner_two = jnp.concatenate([corner_two, swap(corner_two, "yl"), lower_two], 0)
     rows_all = lax.all_gather(row_two, ("yl", "core"), axis=0, tiled=False)
     merged, gathered, corner_two, rows_all = lax.optimization_barrier(
         (merged, gathered, corner_two, rows_all)
@@ -908,14 +917,12 @@
             pltpu.VMEM((2 * NB, 5 * BLK, BLK), F32),
             pltpu.VMEM(panel, F32),
             pltpu.VMEM((36, *block), F32),
-            pltpu.SemaphoreType.DMA((64,)),
+            pltpu.SemaphoreType.DMA((96,)),
         ],
         flops=40_000_000_000,
         out_specs=[VMEM, VMEM, ANY, ANY],
     )
-    lower_two, _ = lax.optimization_barrier((lower_two, gathered))
     gathered_two = lax.all_gather(corner_two, ("core", "front"), axis=0, tiled=False)
-    lower_near = lax.all_gather(lower_two, "front", axis=0, tiled=False)
     places = pltpu.SMEM((2, NB), jnp.int32)
     factor_one, near_mine, near_other, near_late = call(
         rest_kernel,
@@ -931,7 +938,7 @@
         [pltpu.VMEM(panel, F32), pltpu.VMEM((NB, *block), F32)]
         + [pltpu.VMEM(panel, F32)] * 3
         + [pltpu.VMEM(panel, BF16)] * 2
-        + [pltpu.VMEM((36, *block), F32)] * 3
+        + [pltpu.VMEM((36, *block), F32)] * 2
         + [places, places, pltpu.SemaphoreType.DMA((64,))],
         flops=15_000_000_000,
         out_specs=[VMEM, ANY, ANY, ANY],
@@ -963,14 +970,13 @@
         tail_kernel,
         "tail",
         [shape(4 * BLK, BLK), shape(2 * BLK, BLK)],
-        [SMEM, SMEM, ANY, ANY, ANY] + [VMEM] * 3 + [ANY] * 6,
+        [SMEM, SMEM, ANY, ANY, ANY] + [VMEM] * 2 + [ANY] * 6,
         (
             ids,
             parent_map_two,
             gathered_two,
             chol,
             inverse,
-            lower_near,
             rows_all,
             tail_two,
             *packed,
@@ -990,7 +996,7 @@
             pltpu.SMEM((2, FB), jnp.int32),
             places,
             places,
-            pltpu.SemaphoreType.DMA((8,)),
+            pltpu.SemaphoreType.DMA((9,)),
             pltpu.SemaphoreType.DMA((4,)),
         ],
     )

time: 218 us -> 221 us (1.014)
  the two profiles are of different devices: /device:TPU:16 before, /device:TPU:1 now
where the time goes in v3:
time: 221 us; the launch traced here: 219 us
  Pallas kernels  112 us (51%)
  waiting for transfers between devices  75.5 us (34%)
  between operations  13.8 us (6%)
  blocking collectives  10.3 us (5%)
  starting transfers between devices  4.85 us (2%)
    pallas_call x6, Pallas kernels, call(): pl.pallas_call(kernel, name=name, out_shape=outs, in_specs=specs, out_spe...  112 us
    all_gather x1, waiting for transfers between devices, per_device(): gathered = lax.all_gather(sent, ('core', 'front'), axis=0, tiled=False)  49 us
    ppermute x4, waiting for transfers between devices, swap(): return lax.ppermute(value, axis, [(0, 1), (1, 0)])  18.1 us
    all_gather x1, blocking collectives, per_device(): rows_all = lax.all_gather(row_two, ('yl', 'core'), axis=0, tiled=False)  10.3 us
    all_gather x1, waiting for transfers between devices, per_device(): lax.all_gather(corner_two, ('core', 'front'), axis=0, tiled=False)  4.91 us
    ppermute x4, starting transfers between devices, swap(): return lax.ppermute(value, axis, [(0, 1), (1, 0)])  4.73 us
  transfers between devices with their start and end apart: 7, of which 5 were waited for; matrix products, arithmetic and copies ran while one was open for 1% of the time, Pallas kernels for 44%

profile of v3, /device:TPU:1, one launch (start us, length us, event | category | flops | bytes accessed | tf_op | source)
XLA Modules:
  0.0 219.4 jit_solution(17222706719458418097)
XLA Ops:
  7.2 0.0 all-gather.8.cloned.1.call-start
  7.2 0.6 stack.23.ids
  7.8 5.0 %pack.1 = f32[1216,128]{1,0:T(8,128)} custom-call(s32[5]{0:T(128)} %stack.23.ids, s32[16,16,16]{2,1,0:T(8,128)} %pattern_one.3, f32[1024,128]{1,0:T(8,128)} %child_in.1, f32[1024,256]{1,0:T(8,128)} %initial_one.1), custom_call_target="tpu_custom_call" | custom-call | tf_op jit(solution)/shard_map/pack/pallas_call | solution.py:842
  12.8 0.0 all-gather.8.cloned.1.call-update
  12.9 0.0 all-gather.10.cloned.1.call-start
  12.9 4.9 %mask.1 = (f32[512,128]{1,0:T(8,128)}, f32[256,128]{1,0:T(8,128)}, f32[256,128]{1,0:T(8,128)}, f32[256,128]{1,0:T(8,128)}, f32[2,128,128]{2,1,0:T(8,128)}) custom-call(s32[5]{0:T(128)} %stack.23.ids, s32[16,16,16]{2,1,0:T(8,128)} %pattern_one.3, s32[8,16,16]{2,1,0:T(8,128)} %pattern_two.1, f32[1024,256]{1,0:T(8,128)} %initial_one.1, f32[512,256]{1,0:T(8,128)} %initial_two.1), custom_call_target="tpu_custom_call" | custom-call | tf_op jit(solution)/shard_map/mask/pallas_call | solution.py:842
  17.8 2.1 collective-permute-start
  19.9 10.3 %all-gather.1 = f32[1024,128]{1,0:T(8,128)} all-gather(f32[256,128]{1,0:T(8,128)} %get-tuple-element.30), channel_id=3, replica_groups=mesh['x'=4,'yh'=2,'yl'=2,'core'=2,'front'=8] {'yl','core'}, dimensions={0}, use_global_device_ids=true | all-gather | bytes 655360 | tf_op jit(solution)/shard_map/all_gather | solution.py:904
  30.2 0.0 collective-permute-done
  30.2 1.7 pad_maximum_fusion
  31.9 49.0 %all-gather.8.cloned.1.call-done = f32[19456,128]{1,0:T(8,128)} async-done(((f32[1216,128]{1,0:T(8,128)}), f32[19456,128]{1,0:T(8,128)}) %all-gather.8.cloned.1.call-update) | async-done | bytes 9961488 | tf_op jit(solution)/shard_map/all_gather | solution.py:888
  81.0 0.0 all-gather.10.cloned.1.call-update
  81.0 0.0 all-gather.12.cloned.1.call-start
  81.1 0.7 all-gather.12.cloned.1.call-update
  81.7 39.9 %chol.1 = (f32[8,1024,128]{2,1,0:T(8,128)}, f32[8,128,128]{2,1,0:T(8,128)}, f32[8,1024,128]{2,1,0:T(8,128)}, f32[36,128,128]{2,1,0:T(8,128)}) custom-call(s32[5]{0:T(128)} %stack.23.ids, s32[16,2,16]{2,1,0:T(2,128)} %block_map.3, f32[16,1216,128]{2,1,0:T(8,128)} %bitcast.12), custom_call_target="tpu_custom_call" | custom-call | flops 40000000000 | bytes 100000000 | tf_op jit(solution)/shard_map/chol/pallas_call | solution.py:842
  121.6 2.8 %all-gather.10.cloned.1.call-done = f32[8192,128]{1,0:T(8,128)} async-done(((f32[512,128]{1,0:T(8,128)}), f32[8192,128]{1,0:T(8,128)}) %all-gather.10.cloned.1.call-update) | async-done | bytes 4194320 | tf_op jit(solution)/shard_map/all_gather | solution.py:908
  124.4 20.9 %rest.1 = (f32[1024,128]{1,0:T(8,128)}, f32[11,128,128]{2,1,0:T(8,128)}, f32[11,128,128]{2,1,0:T(8,128)}, f32[14,128,128]{2,1,0:T(8,128)}) custom-call(s32[5]{0:T(128)} %stack.23.ids, s32[8,2,16]{2,1,0:T(2,128)} %map_two.1, f32[8,1024,128]{2,1,0:T(8,128)} %get-tuple-element.32.chol_in, f32[8,128,128]{2,1,0:T(8,128)} %get-tuple-element.33.inverse_in, ...), custom_call_target="tpu_custom_call" | custom-call | flops 15000000512 | bytes 37500000 | tf_op jit(solution)/shard_map/rest/pallas_call | solution.py:842
  145.2 0.9 collective-permute-start.1
  146.1 17.0 %collective-permute-done.1.far_mine = f32[11,128,128]{2,1,0:T(8,128)S(1)} collective-permute-done((f32[11,128,128]{2,1,0:T(8,128)}, f32[11,128,128]{2,1,0:T(8,128)S(1)}, u32[]{:S(2)}, u32[]{:S(2)}) %collective-permute-start.1) | collective-permute-done | bytes 720928 | tf_op jit(solution)/shard_map/ppermute | solution.py:857
  163.1 0.0 copy-start.1
  163.1 1.0 collective-permute-start.2
  164.1 0.8 collective-permute-start.3
  164.9 1.0 collective-permute-done.2.far_other
  165.9 0.0 copy-start.2
  165.9 4.9 %all-gather.12.cloned.1.call-done = f32[12288,128]{1,0:T(8,128)} async-done(((f32[768,128]{1,0:T(8,128)}), f32[12288,128]{1,0:T(8,128)}) %all-gather.12.cloned.1.call-update) | async-done | bytes 6291472 | tf_op jit(solution)/shard_map/all_gather | solution.py:925
  170.8 0.0 copy-done.1
  170.8 0.0 copy-done.2
  170.8 30.2 %chol_two.1 = (f32[8,1024,128]{2,1,0:T(8,128)}, f32[8,128,128]{2,1,0:T(8,128)}) custom-call(s32[5]{0:T(128)} %stack.23.ids, s32[8,2,16]{2,1,0:T(2,128)} %map_two.1, f32[16,768,128]{2,1,0:T(8,128)} %bitcast.9, f32[11,128,128]{2,1,0:T(8,128)} %get-tuple-element.39.near_mine, f32[11,128,128]{2,1,0:T(8,128)} %get-tuple-element.40.near_other, ...), custom_call_target="tpu_custom_call" | custom-call | flops 40000000000 | bytes 100000000 | tf_op jit(solution)/shard_map/chol_two/pallas_call | solution.py:842
  201.0 0.0 collective-permute-done.3.far_late
  201.1 0.0 copy-start
  201.1 1.0 copy-done
  202.0 10.9 %tail.1 = (f32[512,128]{1,0:T(8,128)}, f32[256,128]{1,0:T(8,128)}) custom-call(s32[5]{0:T(128)} %stack.23.ids, s32[8,2,16]{2,1,0:T(2,128)} %map_two.1, f32[16,768,128]{2,1,0:T(8,128)} %bitcast.10, f32[8,1024,128]{2,1,0:T(8,128)} %get-tuple-element.41.chol_in, f32[8,128,128]{2,1,0:T(8,128)} %get-tuple-element.42.inverse_in, f32[4,256,128]{2,1,0:T(8,128)} %bitcast.11, ...), custom_call_target="tpu_custom_call" | custom-call | tf_op jit(solution)/shard_map/tail/pallas_call | solution.py:842
Async XLA Ops:
  7.2 73.8 %all-gather.8.cloned.1.call-start = ((), (), s32[]{:S(2)}) async-start(), calls=%async_computation | async-start | bytes 10584064 | tf_op jit(solution)/shard_map/all_gather | solution.py:888
  12.9 111.5 %all-gather.10.cloned.1.call-start = ((), (), s32[]{:S(2)}) async-start(), calls=%async_computation.1 | async-start | bytes 4456448 | tf_op jit(solution)/shard_map/all_gather | solution.py:908
  17.8 12.4 %collective-permute-start = (f32[256,128]{1,0:T(8,128)}, f32[256,128]{1,0:T(8,128)S(1)}, u32[]{:S(2)}, u32[]{:S(2)}) collective-permute-start(f32[256,128]{1,0:T(8,128)} %get-tuple-element.28), channel_id=1, source_target_pairs={{0,16},{16,0},{1,17},{17,1},{2,18},{18,2},{3,19},{19,3},{4,20},{20... | collective-permute-start | bytes 393224 | tf_op jit(solution)/shard_map/ppermute | solution.py:857
  81.0 89.8 %all-gather.12.cloned.1.call-start = ((), (), s32[]{:S(2)}) async-start(), calls=%async_computation.2 | async-start | bytes 6684672 | tf_op jit(solution)/shard_map/all_gather | solution.py:925
  145.2 17.9 %collective-permute-start.1 = (f32[11,128,128]{2,1,0:T(8,128)}, f32[11,128,128]{2,1,0:T(8,128)S(1)}, u32[]{:S(2)}, u32[]{:S(2)}) collective-permute-start(f32[11,128,128]{2,1,0:T(8,128)} %get-tuple-element.39.near_mine), channel_id=1, source_target_pairs={{0,16},{16,0},{1,17},{17,1},{2,18},{18,2},{3,19},{19,3},{4,20},{20... | collective-permute-start | bytes 2162696 | tf_op jit(solution)/shard_map/ppermute | solution.py:857
  163.1 7.7 %copy-start.1 = (f32[11,128,128]{2,1,0:T(8,128)}, f32[11,128,128]{2,1,0:T(8,128)S(1)}, u32[]{:S(2)}) copy-start(f32[11,128,128]{2,1,0:T(8,128)S(1)} %collective-permute-done.1.far_mine) | copy-start | bytes 2162692
  163.1 2.8 %collective-permute-start.2 = (f32[11,128,128]{2,1,0:T(8,128)S(1)}, f32[11,128,128]{2,1,0:T(8,128)S(1)}, u32[]{:S(2)}, u32[]{:S(2)}) collective-permute-start(f32[11,128,128]{2,1,0:T(8,128)S(1)} %collective-permute-done.1.far_mine), channel_id=1, source_target_pairs={{0,8},{8,0},{1,9},{9,1},{2,10},{10,2},{3,11},{11,3},{4,12},{12,4},... | collective-permute-start | bytes 2162696 | tf_op jit(solution)/shard_map/ppermute | solution.py:857
  164.1 36.9 %collective-permute-start.3 = (f32[14,128,128]{2,1,0:T(8,128)}, f32[14,128,128]{2,1,0:T(8,128)S(1)}, u32[]{:S(2)}, u32[]{:S(2)}) collective-permute-start(f32[14,128,128]{2,1,0:T(8,128)} %get-tuple-element.46.near_late), channel_id=1, source_target_pairs={{0,16},{16,0},{1,17},{17,1},{2,18},{18,2},{3,19},{19,3},{4,20},{20... | collective-permute-start | bytes 2752520 | tf_op jit(solution)/shard_map/ppermute | solution.py:857
  165.9 4.9 %copy-start.2 = (f32[11,128,128]{2,1,0:T(8,128)}, f32[11,128,128]{2,1,0:T(8,128)S(1)}, u32[]{:S(2)}) copy-start(f32[11,128,128]{2,1,0:T(8,128)S(1)} %collective-permute-done.2.far_other) | copy-start | bytes 2162692
  201.1 1.0 copy-start
Sparse Core Ops, SparseCore 0:
  13.0 67.9 all-gather.7
  83.4 40.9 all-gather.9
  126.2 44.5 all-gather.11

commit v4 on v2

--- a/solution.py
+++ b/solution.py
@@ -52,13 +52,16 @@
         if t + 1 < last:
             following = lane_columns(rows[t + 1], t + 1)
         scale, weight = [], {}
+        ahead = across(head[0][0:1])
         for b in range(8):
-            pivot = across(head[b][b : b + 1])
+            pivot = ahead
             scale.append(lax.rsqrt(pivot))
             diag = jnp.where(lane == 8 * t + b, pivot * scale[b], diag)
             low = head[b] * scale[b]
             for a in range(b + 1, 8):
-                weight[a, b] = across(low[a : a + 1])
+                weight[a, b] = across(head[b][a : a + 1]) * scale[b]
+                if a == b + 1:
+                    ahead = across(head[a][a : a + 1]) - weight[a, b] * weight[a, b]
                 head[a] = head[a] - low * weight[a, b]
         inside = (lane >= 8 * t) & (lane < 8 * t + 8)
         pivots = []
@@ -451,15 +454,22 @@
     return jnp.where(keep, initial[local * BLK : (local + 1) * BLK, :], 0.0)
 
 
-def pack_kernel(ids, pattern_one, child, initial, merged, columns, tile, sem):
+def pack_kernel(ids, pattern_one, child_in, initial, sent, child, corner, sems):
     front_one, side, z = ids[0], ids[1], ids[2]
-    copy = pltpu.make_async_copy(initial.at[:, :BLK], columns, sem)
-    copy.start()
-    send_child(child, z, merged.at[:CHILD_ROWS, :])
-    copy.wait()
+    copies = [pltpu.make_async_copy(child_in, child, sems.at[4])]
     for r in range(4):
-        tile[r] = masked_tile(columns, pattern_one, front_one, NB * side + 2 * r, 2 * r, 2 * z)
-    send_blocks(tile, side, z, merged.at[CHILD_ROWS:, :])
+        source = initial.at[2 * r * BLK : (2 * r + 1) * BLK, :BLK]
+        copies.append(pltpu.make_async_copy(source, corner.at[r], sems.at[r]))
+    for copy in copies:
+        copy.start()
+    copies[0].wait()
+    send_child(child, z, sent.at[:CHILD_ROWS, :])
+    for copy in copies[1:]:
+        copy.wait()
+    for r in range(4):
+        keep = kept(pattern_one, front_one, NB * side + 2 * r, 2 * z)
+        corner[r] = jnp.where(keep, corner[r], 0.0)
+    send_blocks(corner, side, z, sent.at[CHILD_ROWS:, :])
 
 
 def mask_kernel(
@@ -716,7 +726,6 @@
     gathered,
     chol_in,
     inverse_in,
-    lower_near,
     rows_all,
     tail,
     near_mine,
@@ -752,6 +761,14 @@
             pltpu.make_async_copy(ref, children.at[child, pl.ds(SOON, LATE)], sems.at[4 + n])
         )
         copies[-1].start()
+    copies.append(
+        pltpu.make_async_copy(
+            gathered.at[pl.ds(side * NB, NB), 4 * BLK :, :],
+            lower.at[:, : 2 * BLK, :],
+            sems.at[8],
+        )
+    )
+    copies[-1].start()
     factors = [
         pltpu.make_async_copy(chol_in, chol, sems.at[6]),
         pltpu.make_async_copy(inverse_in, inverse, sems.at[7]),
@@ -761,7 +778,6 @@
     counts = [ordered(map_two, front, child, order, place) for child in range(2)]
     place_of(map_two, front, 0, slots)
     place_of(map_two, front, 1, slots)
-    lower[:, : 2 * BLK, :] = lower_near[...]
     for s in range(4):
         for b in range(2):
             lower[2 * s + b, 2 * BLK :, :] = rows_all[s, b * BLK : (b + 1) * BLK, :]
@@ -871,9 +887,13 @@
         pack_kernel,
         "pack",
         [shape(CHILD_ROWS + CORNER_ROWS, BLK)],
-        [SMEM, SMEM, VMEM, ANY],
+        [SMEM, SMEM, ANY, ANY],
         (ids, pattern_one, child_updates, initial_one),
-        [pltpu.VMEM((NB * BLK, BLK), F32), pltpu.VMEM((4, *block), F32), pltpu.SemaphoreType.DMA],
+        [
+            pltpu.VMEM((NB * BLK, BLK), F32),
+            pltpu.VMEM((4, *block), F32),
+            pltpu.SemaphoreType.DMA((5,)),
+        ],
     )
     gathered = lax.all_gather(sent, ("core", "front"), axis=0, tiled=False)
     ids_mask, _ = lax.optimization_barrier((ids, sent))
@@ -891,7 +911,7 @@
         (ids_mask, pattern_one, pattern_two, initial_one, initial_two),
         [pltpu.VMEM((4, *block), F32)],
     )
-    corner_two = jnp.concatenate([corner_two, swap(corner_two, "yl")], 0)
+    corner_two = jnp.concatenate([corner_two, swap(corner_two, "yl"), lower_two], 0)
     rows_all = lax.all_gather(row_two, ("yl", "core"), axis=0, tiled=False)
     merged, gathered, corner_two, rows_all = lax.optimization_barrier(
         (merged, gathered, corner_two, rows_all)
@@ -913,9 +933,7 @@
         flops=40_000_000_000,
         out_specs=[VMEM, VMEM, ANY, ANY],
     )
-    lower_two, _ = lax.optimization_barrier((lower_two, gathered))
     gathered_two = lax.all_gather(corner_two, ("core", "front"), axis=0, tiled=False)
-    lower_near = lax.all_gather(lower_two, "front", axis=0, tiled=False)
     places = pltpu.SMEM((2, NB), jnp.int32)
     factor_one, near_mine, near_other, near_late = call(
         rest_kernel,
@@ -963,14 +981,13 @@
         tail_kernel,
         "tail",
         [shape(4 * BLK, BLK), shape(2 * BLK, BLK)],
-        [SMEM, SMEM, ANY, ANY, ANY] + [VMEM] * 3 + [ANY] * 6,
+        [SMEM, SMEM, ANY, ANY, ANY] + [VMEM] * 2 + [ANY] * 6,
         (
             ids,
             parent_map_two,
             gathered_two,
             chol,
             inverse,
-            lower_near,
             rows_all,
             tail_two,
             *packed,
@@ -990,7 +1007,7 @@
             pltpu.SMEM((2, FB), jnp.int32),
             places,
             places,
-            pltpu.SemaphoreType.DMA((8,)),
+            pltpu.SemaphoreType.DMA((9,)),
             pltpu.SemaphoreType.DMA((4,)),
         ],
     )

time: 218 us -> 215 us (0.986)
  the two profiles are of different devices: /device:TPU:16 before, /device:TPU:1 now
where the time goes in v4:
time: 215 us; the launch traced here: 214 us
  Pallas kernels  112 us (52%)
  waiting for transfers between devices  68.1 us (32%)
  between operations  13.8 us (6%)
  blocking collectives  10.3 us (5%)
  starting transfers between devices  5.7 us (3%)
  local copies, waits for them, and re-layouts  2.56 us (1%)
    pallas_call x6, Pallas kernels, call(): pl.pallas_call(kernel, name=name, out_shape=outs, in_specs=specs, out_spe...  112 us
    all_gather x1, waiting for transfers between devices, per_device(): gathered = lax.all_gather(sent, ('core', 'front'), axis=0, tiled=False)  36.4 us
    ppermute x4, waiting for transfers between devices, swap(): return lax.ppermute(value, axis, [(0, 1), (1, 0)])  16.6 us
    all_gather x1, blocking collectives, per_device(): rows_all = lax.all_gather(row_two, ('yl', 'core'), axis=0, tiled=False)  10.3 us
    all_gather x1, waiting for transfers between devices, per_device(): merged_all = lax.all_gather(merged, ('core', 'front'), axis=0, tiled=False)  8.91 us
    ppermute x4, starting transfers between devices, swap(): return lax.ppermute(value, axis, [(0, 1), (1, 0)])  5.58 us
    all_gather x1, waiting for transfers between devices, per_device(): lax.all_gather(corner_two, ('core', 'front'), axis=0, tiled=False)  5.46 us
  transfers between devices with their start and end apart: 7, of which 4 were waited for; matrix products, arithmetic and copies ran while one was open for 1% of the time, Pallas kernels for 45%

profile of v4, /device:TPU:1, one launch (start us, length us, event | category | flops | bytes accessed | tf_op | source)
XLA Modules:
  0.0 214.1 jit_solution(1002494577056942023)
XLA Ops:
  7.2 0.0 all-gather.8.cloned.1.call-start
  7.2 0.7 stack.23.ids
  7.9 4.8 %pack.1 = f32[896,128]{1,0:T(8,128)} custom-call(s32[5]{0:T(128)} %stack.23.ids, s32[16,16,16]{2,1,0:T(8,128)} %pattern_one.3, f32[1024,128]{1,0:T(8,128)} %child_in.1, f32[1024,256]{1,0:T(8,128)} %initial_one.1), custom_call_target="tpu_custom_call" | custom-call | tf_op jit(solution)/shard_map/pack/pallas_call | solution.py:853
  12.7 0.0 all-gather.8.cloned.1.call-update
  12.7 0.0 all-gather.10.cloned.1.call-start
  12.8 5.0 %mask.1 = (f32[832,128]{1,0:T(8,128)}, f32[256,128]{1,0:T(8,128)}, f32[256,128]{1,0:T(8,128)}, f32[256,128]{1,0:T(8,128)}, f32[2,128,128]{2,1,0:T(8,128)}) custom-call(s32[5]{0:T(128)} %stack.23.ids, s32[16,16,16]{2,1,0:T(8,128)} %pattern_one.3, s32[8,16,16]{2,1,0:T(8,128)} %pattern_two.1, f32[1024,256]{1,0:T(8,128)} %initial_one.1, f32[512,256]{1,0:T(8,128)} %initial_two.1), custom_call_target="tpu_custom_call" | custom-call | tf_op jit(solution)/shard_map/mask/pallas_call | solution.py:853
  17.8 2.1 collective-permute-start
  19.9 10.3 %all-gather.1 = f32[1024,128]{1,0:T(8,128)} all-gather(f32[256,128]{1,0:T(8,128)} %get-tuple-element.30), channel_id=3, replica_groups=mesh['x'=4,'yh'=2,'yl'=2,'core'=2,'front'=8] {'yl','core'}, dimensions={0}, use_global_device_ids=true | all-gather | bytes 655360 | tf_op jit(solution)/shard_map/all_gather | solution.py:915
  30.2 0.0 collective-permute-done
  30.2 1.8 pad_maximum_fusion
  32.0 36.4 %all-gather.8.cloned.1.call-done = f32[14336,128]{1,0:T(8,128)} async-done(((f32[896,128]{1,0:T(8,128)}), f32[14336,128]{1,0:T(8,128)}) %all-gather.8.cloned.1.call-update) | async-done | bytes 7340048 | tf_op jit(solution)/shard_map/all_gather | solution.py:898
  68.3 0.0 all-gather.10.cloned.1.call-update
  68.4 0.0 all-gather.12.cloned.1.call-start
  68.4 0.7 all-gather.12.cloned.1.call-update
  69.1 39.3 %chol.1 = (f32[8,1024,128]{2,1,0:T(8,128)}, f32[8,128,128]{2,1,0:T(8,128)}, f32[8,1024,128]{2,1,0:T(8,128)}, f32[36,128,128]{2,1,0:T(8,128)}) custom-call(s32[5]{0:T(128)} %stack.23.ids, s32[16,2,16]{2,1,0:T(2,128)} %block_map.3, f32[16,896,128]{2,1,0:T(8,128)} %bitcast.12), custom_call_target="tpu_custom_call" | custom-call | flops 40000000000 | bytes 100000000 | tf_op jit(solution)/shard_map/chol/pallas_call | solution.py:853
  108.4 8.9 %all-gather.10.cloned.1.call-done = f32[13312,128]{1,0:T(8,128)} async-done(((f32[832,128]{1,0:T(8,128)}), f32[13312,128]{1,0:T(8,128)}) %all-gather.10.cloned.1.call-update) | async-done | bytes 6815760 | tf_op jit(solution)/shard_map/all_gather | solution.py:919
  117.3 21.0 %rest.1 = (f32[1024,128]{1,0:T(8,128)}, f32[11,128,128]{2,1,0:T(8,128)}, f32[11,128,128]{2,1,0:T(8,128)}, f32[14,128,128]{2,1,0:T(8,128)}) custom-call(s32[5]{0:T(128)} %stack.23.ids, s32[8,2,16]{2,1,0:T(2,128)} %map_two.1, f32[8,1024,128]{2,1,0:T(8,128)} %get-tuple-element.32.chol_in, f32[8,128,128]{2,1,0:T(8,128)} %get-tuple-element.33.inverse_in, ...), custom_call_target="tpu_custom_call" | custom-call | flops 15000000512 | bytes 37500000 | tf_op jit(solution)/shard_map/rest/pallas_call | solution.py:853
  138.2 1.3 collective-permute-start.1
  139.5 16.6 %collective-permute-done.1.far_mine = f32[11,128,128]{2,1,0:T(8,128)S(1)} collective-permute-done((f32[11,128,128]{2,1,0:T(8,128)}, f32[11,128,128]{2,1,0:T(8,128)S(1)}, u32[]{:S(2)}, u32[]{:S(2)}) %collective-permute-start.1) | collective-permute-done | bytes 720928 | tf_op jit(solution)/shard_map/ppermute | solution.py:868
  156.1 0.0 copy-start.1
  156.1 1.0 collective-permute-start.2
  157.1 1.2 collective-permute-start.3
  158.3 5.5 %all-gather.12.cloned.1.call-done = f32[12288,128]{1,0:T(8,128)} async-done(((f32[768,128]{1,0:T(8,128)}), f32[12288,128]{1,0:T(8,128)}) %all-gather.12.cloned.1.call-update) | async-done | bytes 6291472 | tf_op jit(solution)/shard_map/all_gather | solution.py:936
  163.8 0.0 collective-permute-done.2.far_other
  163.8 0.0 copy-start.2
  163.8 0.0 copy-done.1
  163.8 0.9 copy-done.2
  164.7 31.4 %chol_two.1 = (f32[8,1024,128]{2,1,0:T(8,128)}, f32[8,128,128]{2,1,0:T(8,128)}) custom-call(s32[5]{0:T(128)} %stack.23.ids, s32[8,2,16]{2,1,0:T(2,128)} %map_two.1, f32[16,768,128]{2,1,0:T(8,128)} %bitcast.9, f32[11,128,128]{2,1,0:T(8,128)} %get-tuple-element.39.near_mine, f32[11,128,128]{2,1,0:T(8,128)} %get-tuple-element.40.near_other, ...), custom_call_target="tpu_custom_call" | custom-call | flops 40000000000 | bytes 100000000 | tf_op jit(solution)/shard_map/chol_two/pallas_call | solution.py:853
  196.1 0.0 collective-permute-done.3.far_late
  196.1 0.0 copy-start
  196.1 1.0 copy-done
  197.1 10.5 %tail.1 = (f32[512,128]{1,0:T(8,128)}, f32[256,128]{1,0:T(8,128)}) custom-call(s32[5]{0:T(128)} %stack.23.ids, s32[8,2,16]{2,1,0:T(2,128)} %map_two.1, f32[16,768,128]{2,1,0:T(8,128)} %bitcast.10, f32[8,1024,128]{2,1,0:T(8,128)} %get-tuple-element.41.chol_in, f32[8,128,128]{2,1,0:T(8,128)} %get-tuple-element.42.inverse_in, f32[4,256,128]{2,1,0:T(8,128)} %bitcast.11, ...), custom_call_target="tpu_custom_call" | custom-call | tf_op jit(solution)/shard_map/tail/pallas_call | solution.py:853
Async XLA Ops:
  7.2 61.2 %all-gather.8.cloned.1.call-start = ((), (), s32[]{:S(2)}) async-start(), calls=%async_computation | async-start | bytes 7798784 | tf_op jit(solution)/shard_map/all_gather | solution.py:898
  12.7 104.5 %all-gather.10.cloned.1.call-start = ((), (), s32[]{:S(2)}) async-start(), calls=%async_computation.1 | async-start | bytes 7241728 | tf_op jit(solution)/shard_map/all_gather | solution.py:919
  17.8 12.4 %collective-permute-start = (f32[256,128]{1,0:T(8,128)}, f32[256,128]{1,0:T(8,128)S(1)}, u32[]{:S(2)}, u32[]{:S(2)}) collective-permute-start(f32[256,128]{1,0:T(8,128)} %get-tuple-element.28), channel_id=1, source_target_pairs={{0,16},{16,0},{1,17},{17,1},{2,18},{18,2},{3,19},{19,3},{4,20},{20... | collective-permute-start | bytes 393224 | tf_op jit(solution)/shard_map/ppermute | solution.py:868
  68.4 95.4 %all-gather.12.cloned.1.call-start = ((), (), s32[]{:S(2)}) async-start(), calls=%async_computation.2 | async-start | bytes 6684672 | tf_op jit(solution)/shard_map/all_gather | solution.py:936
  138.2 17.9 %collective-permute-start.1 = (f32[11,128,128]{2,1,0:T(8,128)}, f32[11,128,128]{2,1,0:T(8,128)S(1)}, u32[]{:S(2)}, u32[]{:S(2)}) collective-permute-start(f32[11,128,128]{2,1,0:T(8,128)} %get-tuple-element.39.near_mine), channel_id=1, source_target_pairs={{0,16},{16,0},{1,17},{17,1},{2,18},{18,2},{3,19},{19,3},{4,20},{20... | collective-permute-start | bytes 2162696 | tf_op jit(solution)/shard_map/ppermute | solution.py:868
  156.1 7.6 %copy-start.1 = (f32[11,128,128]{2,1,0:T(8,128)}, f32[11,128,128]{2,1,0:T(8,128)S(1)}, u32[]{:S(2)}) copy-start(f32[11,128,128]{2,1,0:T(8,128)S(1)} %collective-permute-done.1.far_mine) | copy-start | bytes 2162692
  156.1 7.6 %collective-permute-start.2 = (f32[11,128,128]{2,1,0:T(8,128)S(1)}, f32[11,128,128]{2,1,0:T(8,128)S(1)}, u32[]{:S(2)}, u32[]{:S(2)}) collective-permute-start(f32[11,128,128]{2,1,0:T(8,128)S(1)} %collective-permute-done.1.far_mine), channel_id=1, source_target_pairs={{0,8},{8,0},{1,9},{9,1},{2,10},{10,2},{3,11},{11,3},{4,12},{12,4},... | collective-permute-start | bytes 2162696 | tf_op jit(solution)/shard_map/ppermute | solution.py:868
  157.1 39.0 %collective-permute-start.3 = (f32[14,128,128]{2,1,0:T(8,128)}, f32[14,128,128]{2,1,0:T(8,128)S(1)}, u32[]{:S(2)}, u32[]{:S(2)}) collective-permute-start(f32[14,128,128]{2,1,0:T(8,128)} %get-tuple-element.46.near_late), channel_id=1, source_target_pairs={{0,16},{16,0},{1,17},{17,1},{2,18},{18,2},{3,19},{19,3},{4,20},{20... | collective-permute-start | bytes 2752520 | tf_op jit(solution)/shard_map/ppermute | solution.py:868
  163.8 0.9 copy-start.2
  196.1 1.0 copy-start
Sparse Core Ops, SparseCore 0:
  12.9 55.4 all-gather.7
  70.2 47.0 all-gather.9
  119.1 44.5 all-gather.11

commit v5 on v4

--- a/solution.py
+++ b/solution.py
@@ -22,6 +22,7 @@
 MOST = 6
 SOON = 22
 LATE = 36 - SOON
+PAIR_ROWS = BLK + HALF
 
 
 def shape(*dims):
@@ -449,6 +450,30 @@
     return visit
 
 
+def sent_row(sub, z):
+    return jnp.where(sub >= z // 2, z % 2, 1 - z % 2)
+
+
+def send_pair(tile, sub, z, out):
+    block = tile[sent_row(sub, z)]
+
+    @pl.when(2 * sub + sent_row(sub, z) >= z)
+    def _():
+        out[:BLK, :] = block
+
+    @pl.when(2 * sub + sent_row(sub, z) < z)
+    def _():
+        out[:BLK, :] = block.T
+
+    @pl.when(z % 2 == 0)
+    def _():
+        out[BLK:, :] = tile[1][:HALF, :]
+
+    @pl.when(z % 2 == 1)
+    def _():
+        out[BLK:, :] = tile[0].T[HALF:, :]
+
+
 def masked_tile(initial, pattern, front, row, local, col):
     keep = kept(pattern, front, row, col)
     return jnp.where(keep, initial[local * BLK : (local + 1) * BLK, :], 0.0)
@@ -484,6 +509,7 @@
     row_two,
     tail_two,
     tile,
+    corner_tile,
 ):
     front_one, side, z, front_two, sub = ids[0], ids[1], ids[2], ids[3], ids[4]
     first, second = initial_one.at[:, :BLK], initial_one.at[:, BLK:]
@@ -499,12 +525,15 @@
             columns = initial_two.at[:, w * BLK : (w + 1) * BLK]
             block = masked_tile(columns, pattern_two, front_two, 4 * sub + r, r, 2 * z + w)
             at = slice(r // 2 * BLK, (r // 2 + 1) * BLK)
-            if w == 0:
-                (corner_two if r % 2 == 0 else lower_two)[at, :] = block
+            if w == 0 and r % 2 == 0:
+                corner_tile[r // 2] = block
+            elif w == 0:
+                lower_two[at, :] = block
             elif r % 2 == 0:
                 row_two[at, :] = block.T
             else:
                 tail_two[r // 2] = block
+    send_pair(corner_tile, sub, z, corner_two)
 
 
 def chol_kernel(
@@ -675,17 +704,28 @@
 
 def corner_copies(side_of, gathered, work, sems):
     copies = []
+
+    def fetch(piece, first, rows, block_row, block_col, start):
+        place = pl.multiple_of(block_row * BLK + start, HALF)
+        copies.append(
+            pltpu.make_async_copy(
+                gathered.at[piece, first : first + rows, :],
+                work.at[block_col, pl.ds(place, rows), :],
+                sems.at[len(copies)],
+            )
+        )
+        copies[-1].start()
+
     for core in range(2):
         for n, y in ((0, side_of), (1, 1 - side_of)):
-            start = pl.multiple_of(2 * (2 * y + core) * BLK, BLK)
-            copies.append(
-                pltpu.make_async_copy(
-                    gathered.at[core * NB : (core + 1) * NB, 2 * n * BLK : 2 * (n + 1) * BLK, :],
-                    work.at[:, pl.ds(start, 2 * BLK), :],
-                    sems.at[2 * core + n],
-                )
-            )
-            copies[-1].start()
+            sub = 2 * y + core
+            for z in range(NB):
+                row = 2 * sub + sent_row(sub, z)
+                top, left = jnp.maximum(row, z), jnp.minimum(row, z)
+                fetch(core * NB + z, n * PAIR_ROWS, BLK, top, left, 0)
+            for d in range(2):
+                piece = core * NB + 2 * sub + d
+                fetch(piece, n * PAIR_ROWS + BLK, HALF, 2 * sub + 1, 2 * sub, d * HALF)
     return copies
 
 
@@ -763,7 +803,7 @@
         copies[-1].start()
     copies.append(
         pltpu.make_async_copy(
-            gathered.at[pl.ds(side * NB, NB), 4 * BLK :, :],
+            gathered.at[pl.ds(side * NB, NB), 2 * PAIR_ROWS :, :],
             lower.at[:, : 2 * BLK, :],
             sems.at[8],
         )
@@ -902,14 +942,14 @@
         "mask",
         [
             shape(LOWER_ROWS + CORNER_ROWS, BLK),
-            shape(2 * BLK, BLK),
+            shape(PAIR_ROWS, BLK),
             shape(2 * BLK, BLK),
             shape(2 * BLK, BLK),
             shape(2, *block),
         ],
         [SMEM, SMEM, SMEM, VMEM, VMEM],
         (ids_mask, pattern_one, pattern_two, initial_one, initial_two),
-        [pltpu.VMEM((4, *block), F32)],
+        [pltpu.VMEM((4, *block), F32), pltpu.VMEM((2, *block), F32)],
     )
     corner_two = jnp.concatenate([corner_two, swap(corner_two, "yl"), lower_two], 0)
     rows_all = lax.all_gather(row_two, ("yl", "core"), axis=0, tiled=False)
@@ -972,7 +1012,7 @@
             places,
             places,
             pltpu.SemaphoreType.DMA((4,)),
-            pltpu.SemaphoreType.DMA((4,)),
+            pltpu.SemaphoreType.DMA((40,)),
         ],
         flops=40_000_000_000,
     )
@@ -1008,7 +1048,7 @@
             places,
             places,
             pltpu.SemaphoreType.DMA((9,)),
-            pltpu.SemaphoreType.DMA((4,)),
+            pltpu.SemaphoreType.DMA((40,)),
         ],
     )
     return factor_one, factor_two, schur_two

time: 215 us -> 213 us (level)
    all_gather x1, waiting for transfers between devices: 5.46 us -> 2.81 us  [per_device(): lax.all_gather(corner_two, ('core', 'front'), axis=0, tiled=False)]
where the time goes in v5:
time: 213 us; the launch traced here: 212 us
  Pallas kernels  112 us (53%)
  waiting for transfers between devices  66.6 us (31%)
  between operations  13.8 us (6%)
  blocking collectives  9.94 us (5%)
  starting transfers between devices  5.68 us (3%)
  local copies, waits for them, and re-layouts  2.41 us (1%)
    pallas_call x6, Pallas kernels, call(): pl.pallas_call(kernel, name=name, out_shape=outs, in_specs=specs, out_spe...  112 us
    all_gather x1, waiting for transfers between devices, per_device(): gathered = lax.all_gather(sent, ('core', 'front'), axis=0, tiled=False)  36.7 us
    ppermute x4, waiting for transfers between devices, swap(): return lax.ppermute(value, axis, [(0, 1), (1, 0)])  16.6 us
    all_gather x1, blocking collectives, per_device(): rows_all = lax.all_gather(row_two, ('yl', 'core'), axis=0, tiled=False)  9.94 us
    all_gather x1, waiting for transfers between devices, per_device(): merged_all = lax.all_gather(merged, ('core', 'front'), axis=0, tiled=False)  9.82 us
    ppermute x4, starting transfers between devices, swap(): return lax.ppermute(value, axis, [(0, 1), (1, 0)])  5.56 us
  transfers between devices with their start and end apart: 7, of which 4 were waited for; matrix products, arithmetic and copies ran while one was open for 1% of the time, Pallas kernels for 45%

profile of v5, /device:TPU:1, one launch (start us, length us, event | category | flops | bytes accessed | tf_op | source)
XLA Modules:
  0.0 212.5 jit_solution(8435537419987455766)
XLA Ops:
  7.2 0.0 all-gather.8.cloned.1.call-start
  7.2 0.6 stack.23.ids
  7.8 4.8 %pack.1 = f32[896,128]{1,0:T(8,128)} custom-call(s32[5]{0:T(128)} %stack.23.ids, s32[16,16,16]{2,1,0:T(8,128)} %pattern_one.3, f32[1024,128]{1,0:T(8,128)} %child_in.1, f32[1024,256]{1,0:T(8,128)} %initial_one.1), custom_call_target="tpu_custom_call" | custom-call | tf_op jit(solution)/shard_map/pack/pallas_call | solution.py:893
  12.6 0.0 all-gather.8.cloned.1.call-update
  12.7 0.0 all-gather.10.cloned.1.call-start
  12.7 5.1 %mask.1 = (f32[832,128]{1,0:T(8,128)}, f32[192,128]{1,0:T(8,128)}, f32[256,128]{1,0:T(8,128)}, f32[256,128]{1,0:T(8,128)}, f32[2,128,128]{2,1,0:T(8,128)}) custom-call(s32[5]{0:T(128)} %stack.23.ids, s32[16,16,16]{2,1,0:T(8,128)} %pattern_one.3, s32[8,16,16]{2,1,0:T(8,128)} %pattern_two.1, f32[1024,256]{1,0:T(8,128)} %initial_one.1, f32[512,256]{1,0:T(8,128)} %initial_two.1), custom_call_target="tpu_custom_call" | custom-call | tf_op jit(solution)/shard_map/mask/pallas_call | solution.py:893
  17.8 2.1 %collective-permute-start = (f32[192,128]{1,0:T(8,128)}, f32[192,128]{1,0:T(8,128)S(1)}, u32[]{:S(2)}, u32[]{:S(2)}) collective-permute-start(f32[192,128]{1,0:T(8,128)} %get-tuple-element.28), channel_id=1, source_target_pairs={{0,16},{16,0},{1,17},{17,1},{2,18},{18,2},{3,19},{19,3},{4,20},{20... | collective-permute-start | bytes 294920 | tf_op jit(solution)/shard_map/ppermute | solution.py:908
  19.9 9.9 %all-gather.1 = f32[1024,128]{1,0:T(8,128)} all-gather(f32[256,128]{1,0:T(8,128)} %get-tuple-element.30), channel_id=3, replica_groups=mesh['x'=4,'yh'=2,'yl'=2,'core'=2,'front'=8] {'yl','core'}, dimensions={0}, use_global_device_ids=true | all-gather | bytes 655360 | tf_op jit(solution)/shard_map/all_gather | solution.py:955
  29.9 0.0 collective-permute-done
  29.9 1.7 pad_maximum_fusion
  31.6 36.7 %all-gather.8.cloned.1.call-done = f32[14336,128]{1,0:T(8,128)} async-done(((f32[896,128]{1,0:T(8,128)}), f32[14336,128]{1,0:T(8,128)}) %all-gather.8.cloned.1.call-update) | async-done | bytes 7340048 | tf_op jit(solution)/shard_map/all_gather | solution.py:938
  68.3 0.0 all-gather.10.cloned.1.call-update
  68.3 0.0 all-gather.12.cloned.1.call-start
  68.3 0.7 all-gather.12.cloned.1.call-update
  69.0 38.4 %chol.1 = (f32[8,1024,128]{2,1,0:T(8,128)}, f32[8,128,128]{2,1,0:T(8,128)}, f32[8,1024,128]{2,1,0:T(8,128)}, f32[36,128,128]{2,1,0:T(8,128)}) custom-call(s32[5]{0:T(128)} %stack.23.ids, s32[16,2,16]{2,1,0:T(2,128)} %block_map.3, f32[16,896,128]{2,1,0:T(8,128)} %bitcast.12), custom_call_target="tpu_custom_call" | custom-call | flops 40000000000 | bytes 100000000 | tf_op jit(solution)/shard_map/chol/pallas_call | solution.py:893
  107.4 9.8 %all-gather.10.cloned.1.call-done = f32[13312,128]{1,0:T(8,128)} async-done(((f32[832,128]{1,0:T(8,128)}), f32[13312,128]{1,0:T(8,128)}) %all-gather.10.cloned.1.call-update) | async-done | bytes 6815760 | tf_op jit(solution)/shard_map/all_gather | solution.py:959
  117.2 21.0 %rest.1 = (f32[1024,128]{1,0:T(8,128)}, f32[11,128,128]{2,1,0:T(8,128)}, f32[11,128,128]{2,1,0:T(8,128)}, f32[14,128,128]{2,1,0:T(8,128)}) custom-call(s32[5]{0:T(128)} %stack.23.ids, s32[8,2,16]{2,1,0:T(2,128)} %map_two.1, f32[8,1024,128]{2,1,0:T(8,128)} %get-tuple-element.32.chol_in, f32[8,128,128]{2,1,0:T(8,128)} %get-tuple-element.33.inverse_in, ...), custom_call_target="tpu_custom_call" | custom-call | flops 15000000512 | bytes 37500000 | tf_op jit(solution)/shard_map/rest/pallas_call | solution.py:893
  138.2 1.3 collective-permute-start.1
  139.5 16.6 %collective-permute-done.1.far_mine = f32[11,128,128]{2,1,0:T(8,128)S(1)} collective-permute-done((f32[11,128,128]{2,1,0:T(8,128)}, f32[11,128,128]{2,1,0:T(8,128)S(1)}, u32[]{:S(2)}, u32[]{:S(2)}) %collective-permute-start.1) | collective-permute-done | bytes 720928 | tf_op jit(solution)/shard_map/ppermute | solution.py:908
  156.1 0.0 copy-start.1
  156.1 1.0 collective-permute-start.2
  157.1 1.2 collective-permute-start.3
  158.3 2.8 %all-gather.12.cloned.1.call-done = f32[10240,128]{1,0:T(8,128)} async-done(((f32[640,128]{1,0:T(8,128)}), f32[10240,128]{1,0:T(8,128)}) %all-gather.12.cloned.1.call-update) | async-done | bytes 5242896 | tf_op jit(solution)/shard_map/all_gather | solution.py:976
  161.1 0.0 collective-permute-done.2.far_other
  161.1 0.0 copy-start.2
  161.1 0.0 copy-done.1
  161.1 0.9 copy-done.2
  162.0 31.5 %chol_two.1 = (f32[8,1024,128]{2,1,0:T(8,128)}, f32[8,128,128]{2,1,0:T(8,128)}) custom-call(s32[5]{0:T(128)} %stack.23.ids, s32[8,2,16]{2,1,0:T(2,128)} %map_two.1, f32[16,640,128]{2,1,0:T(8,128)} %bitcast.9, f32[11,128,128]{2,1,0:T(8,128)} %get-tuple-element.39.near_mine, f32[11,128,128]{2,1,0:T(8,128)} %get-tuple-element.40.near_other, ...), custom_call_target="tpu_custom_call" | custom-call | flops 40000000000 | bytes 100000000 | tf_op jit(solution)/shard_map/chol_two/pallas_call | solution.py:893
  193.5 0.0 collective-permute-done.3.far_late
  193.5 0.0 copy-start
  193.5 0.9 copy-done
  194.4 11.5 %tail.1 = (f32[512,128]{1,0:T(8,128)}, f32[256,128]{1,0:T(8,128)}) custom-call(s32[5]{0:T(128)} %stack.23.ids, s32[8,2,16]{2,1,0:T(2,128)} %map_two.1, f32[16,640,128]{2,1,0:T(8,128)} %bitcast.10, f32[8,1024,128]{2,1,0:T(8,128)} %get-tuple-element.41.chol_in, f32[8,128,128]{2,1,0:T(8,128)} %get-tuple-element.42.inverse_in, f32[4,256,128]{2,1,0:T(8,128)} %bitcast.11, ...), custom_call_target="tpu_custom_call" | custom-call | tf_op jit(solution)/shard_map/tail/pallas_call | solution.py:893
Async XLA Ops:
  7.2 61.1 %all-gather.8.cloned.1.call-start = ((), (), s32[]{:S(2)}) async-start(), calls=%async_computation | async-start | bytes 7798784 | tf_op jit(solution)/shard_map/all_gather | solution.py:938
  12.7 104.6 %all-gather.10.cloned.1.call-start = ((), (), s32[]{:S(2)}) async-start(), calls=%async_computation.1 | async-start | bytes 7241728 | tf_op jit(solution)/shard_map/all_gather | solution.py:959
  17.8 12.1 %collective-permute-start = (f32[192,128]{1,0:T(8,128)}, f32[192,128]{1,0:T(8,128)S(1)}, u32[]{:S(2)}, u32[]{:S(2)}) collective-permute-start(f32[192,128]{1,0:T(8,128)} %get-tuple-element.28), channel_id=1, source_target_pairs={{0,16},{16,0},{1,17},{17,1},{2,18},{18,2},{3,19},{19,3},{4,20},{20... | collective-permute-start | bytes 294920 | tf_op jit(solution)/shard_map/ppermute | solution.py:908
  68.3 92.8 %all-gather.12.cloned.1.call-start = ((), (), s32[]{:S(2)}) async-start(), calls=%async_computation.2 | async-start | bytes 5570560 | tf_op jit(solution)/shard_map/all_gather | solution.py:976
  138.2 17.9 %collective-permute-start.1 = (f32[11,128,128]{2,1,0:T(8,128)}, f32[11,128,128]{2,1,0:T(8,128)S(1)}, u32[]{:S(2)}, u32[]{:S(2)}) collective-permute-start(f32[11,128,128]{2,1,0:T(8,128)} %get-tuple-element.39.near_mine), channel_id=1, source_target_pairs={{0,16},{16,0},{1,17},{17,1},{2,18},{18,2},{3,19},{19,3},{4,20},{20... | collective-permute-start | bytes 2162696 | tf_op jit(solution)/shard_map/ppermute | solution.py:908
  156.1 5.0 %copy-start.1 = (f32[11,128,128]{2,1,0:T(8,128)}, f32[11,128,128]{2,1,0:T(8,128)S(1)}, u32[]{:S(2)}) copy-start(f32[11,128,128]{2,1,0:T(8,128)S(1)} %collective-permute-done.1.far_mine) | copy-start | bytes 2162692
  156.1 5.0 %collective-permute-start.2 = (f32[11,128,128]{2,1,0:T(8,128)S(1)}, f32[11,128,128]{2,1,0:T(8,128)S(1)}, u32[]{:S(2)}, u32[]{:S(2)}) collective-permute-start(f32[11,128,128]{2,1,0:T(8,128)S(1)} %collective-permute-done.1.far_mine), channel_id=1, source_target_pairs={{0,8},{8,0},{1,9},{9,1},{2,10},{10,2},{3,11},{11,3},{4,12},{12,4},... | collective-permute-start | bytes 2162696 | tf_op jit(solution)/shard_map/ppermute | solution.py:908
  157.1 36.4 %collective-permute-start.3 = (f32[14,128,128]{2,1,0:T(8,128)}, f32[14,128,128]{2,1,0:T(8,128)S(1)}, u32[]{:S(2)}, u32[]{:S(2)}) collective-permute-start(f32[14,128,128]{2,1,0:T(8,128)} %get-tuple-element.46.near_late), channel_id=1, source_target_pairs={{0,16},{16,0},{1,17},{17,1},{2,18},{18,2},{3,19},{19,3},{4,20},{20... | collective-permute-start | bytes 2752520 | tf_op jit(solution)/shard_map/ppermute | solution.py:908
  161.1 0.9 copy-start.2
  193.5 0.9 copy-start
Sparse Core Ops, SparseCore 0:
  12.8 55.4 all-gather.7
  70.1 47.1 all-gather.9
  119.1 41.9 all-gather.11

commit v6 on v5

--- a/solution.py
+++ b/solution.py
@@ -210,7 +210,19 @@
     lax.fori_loop(0, NB, one_panel, 0)
 
 
-def solve_rows(right_side, chol, inverse, solved, solved_high, solved_low):
+def inverse_of_pair(chol, inverse, p):
+    between = chol[p, (p + 1) * BLK : (p + 2) * BLK, :]
+    corner = -dot_split(inverse[p + 1], dot_split(inverse[p].T, between))
+    return jnp.concatenate(
+        [
+            jnp.concatenate([inverse[p], jnp.zeros((BLK, BLK), F32)], 1),
+            jnp.concatenate([corner, inverse[p + 1]], 1),
+        ],
+        0,
+    )
+
+
+def solve_rows(right_side, chol, inverse, solved, solved_high, solved_low, pairs=None):
     for p in range(0, NB, 2):
         value = right_side(p)
         if p:
@@ -224,15 +236,7 @@
                 + dot_nt(left_high, right_low)
                 + dot_nt(left_low, right_high)
             )
-        between = chol[p, (p + 1) * BLK : (p + 2) * BLK, :]
-        corner = -dot_split(inverse[p + 1], dot_split(inverse[p].T, between))
-        pair_inverse = jnp.concatenate(
-            [
-                jnp.concatenate([inverse[p], jnp.zeros((BLK, BLK), F32)], 1),
-                jnp.concatenate([corner, inverse[p + 1]], 1),
-            ],
-            0,
-        )
+        pair_inverse = pairs[p // 2] if pairs is not None else inverse_of_pair(chol, inverse, p)
         value = dot_split(value, pair_inverse)
         high, low = halves(value)
         for w in range(2):
@@ -541,13 +545,14 @@
     block_map,
     gathered,
     chol,
-    inverse,
+    pairs,
     lower_out,
     trail_out,
     work,
     children,
     lower,
     trail,
+    inverse,
     sems,
 ):
     front = ids[0]
@@ -577,6 +582,8 @@
     for copy in outs:
         copy.start()
     factor_corner(work, chol, inverse)
+    for p in range(0, NB, 2):
+        pairs[p // 2] = inverse_of_pair(chol, inverse, p)
     for copy in outs:
         copy.wait()
 
@@ -585,7 +592,7 @@
     ids,
     block_map,
     chol_in,
-    inverse_in,
+    pairs_in,
     lower_in,
     trail_in,
     merged,
@@ -594,7 +601,7 @@
     other,
     late,
     chol,
-    inverse,
+    pairs,
     lower,
     lower_add,
     solved,
@@ -617,7 +624,7 @@
         used.append(copy)
         return copy
 
-    first = [fetch(inverse_in, inverse)]
+    first = [fetch(pairs_in, pairs)]
     columns = {}
     for p in range(0, NB, 2):
         columns[p] = [fetch(lower_in.at[p : p + 2], lower_add.at[p : p + 2])]
@@ -650,7 +657,7 @@
             copy.wait()
         return pair(lower, p) + pair(lower_add, p)
 
-    solve_rows(right_side, chol, inverse, solved, solved_high, solved_low)
+    solve_rows(right_side, chol, None, solved, solved_high, solved_low, pairs)
     for copy in last:
         copy.wait()
     for p in range(0, NB, 2):
@@ -957,10 +964,10 @@
         (merged, gathered, corner_two, rows_all)
     )
     merged_all = lax.all_gather(merged, ("core", "front"), axis=0, tiled=False)
-    chol, inverse, lower_add, trail_add = call(
+    chol, pairs, lower_add, trail_add = call(
         chol_kernel,
         "chol",
-        [shape(*panel), shape(NB, *block), shape(*panel), shape(36, *block)],
+        [shape(*panel), shape(4, 2 * BLK, 2 * BLK), shape(*panel), shape(36, *block)],
         [SMEM, SMEM, ANY],
         (ids, parent_map_one, gathered),
         [
@@ -968,6 +975,7 @@
             pltpu.VMEM((2 * NB, 5 * BLK, BLK), F32),
             pltpu.VMEM(panel, F32),
             pltpu.VMEM((36, *block), F32),
+            pltpu.VMEM((NB, *block), F32),
             pltpu.SemaphoreType.DMA((64,)),
         ],
         flops=40_000_000_000,
@@ -985,8 +993,8 @@
             shape(LATE, *block),
         ],
         [SMEM, SMEM] + [ANY] * 5,
-        (ids, parent_map_two, chol, inverse, lower_add, trail_add, merged_all),
-        [pltpu.VMEM(panel, F32), pltpu.VMEM((NB, *block), F32)]
+        (ids, parent_map_two, chol, pairs, lower_add, trail_add, merged_all),
+        [pltpu.VMEM(panel, F32), pltpu.VMEM((4, 2 * BLK, 2 * BLK), F32)]
         + [pltpu.VMEM(panel, F32)] * 3
         + [pltpu.VMEM(panel, BF16)] * 2
         + [pltpu.VMEM((36, *block), F32)] * 3

time: 213 us -> 212 us (level)
  no operation moved by 1% of the time
where the time goes in v6:
time: 212 us; the launch traced here: 211 us
  Pallas kernels  111 us (52%)
  waiting for transfers between devices  65.9 us (31%)
  between operations  13.8 us (7%)
  blocking collectives  9.94 us (5%)
  starting transfers between devices  5.71 us (3%)
  local copies, waits for them, and re-layouts  2.41 us (1%)
    pallas_call x6, Pallas kernels, call(): pl.pallas_call(kernel, name=name, out_shape=outs, in_specs=specs, out_spe...  111 us
    all_gather x1, waiting for transfers between devices, per_device(): gathered = lax.all_gather(sent, ('core', 'front'), axis=0, tiled=False)  36.7 us
    ppermute x4, waiting for transfers between devices, swap(): return lax.ppermute(value, axis, [(0, 1), (1, 0)])  16.6 us
    all_gather x1, blocking collectives, per_device(): rows_all = lax.all_gather(row_two, ('yl', 'core'), axis=0, tiled=False)  9.94 us
    all_gather x1, waiting for transfers between devices, per_device(): merged_all = lax.all_gather(merged, ('core', 'front'), axis=0, tiled=False)  8.71 us
    ppermute x4, starting transfers between devices, swap(): return lax.ppermute(value, axis, [(0, 1), (1, 0)])  5.59 us
  transfers between devices with their start and end apart: 7, of which 4 were waited for; matrix products, arithmetic and copies ran while one was open for 1% of the time, Pallas kernels for 45%

profile of v6, /device:TPU:1, one launch (start us, length us, event | category | flops | bytes accessed | tf_op | source)
XLA Modules:
  0.0 210.9 jit_solution(11104583688017178559)
XLA Ops:
  7.2 0.0 all-gather.8.cloned.1.call-start
  7.2 0.6 stack.23.ids
  7.8 4.8 %pack.1 = f32[896,128]{1,0:T(8,128)} custom-call(s32[5]{0:T(128)} %stack.23.ids, s32[16,16,16]{2,1,0:T(8,128)} %pattern_one.3, f32[1024,128]{1,0:T(8,128)} %child_in.1, f32[1024,256]{1,0:T(8,128)} %initial_one.1), custom_call_target="tpu_custom_call" | custom-call | tf_op jit(solution)/shard_map/pack/pallas_call | solution.py:900
  12.6 0.0 all-gather.8.cloned.1.call-update
  12.7 0.0 all-gather.10.cloned.1.call-start
  12.7 5.1 %mask.1 = (f32[832,128]{1,0:T(8,128)}, f32[192,128]{1,0:T(8,128)}, f32[256,128]{1,0:T(8,128)}, f32[256,128]{1,0:T(8,128)}, f32[2,128,128]{2,1,0:T(8,128)}) custom-call(s32[5]{0:T(128)} %stack.23.ids, s32[16,16,16]{2,1,0:T(8,128)} %pattern_one.3, s32[8,16,16]{2,1,0:T(8,128)} %pattern_two.1, f32[1024,256]{1,0:T(8,128)} %initial_one.1, f32[512,256]{1,0:T(8,128)} %initial_two.1), custom_call_target="tpu_custom_call" | custom-call | tf_op jit(solution)/shard_map/mask/pallas_call | solution.py:900
  17.8 2.1 %collective-permute-start = (f32[192,128]{1,0:T(8,128)}, f32[192,128]{1,0:T(8,128)S(1)}, u32[]{:S(2)}, u32[]{:S(2)}) collective-permute-start(f32[192,128]{1,0:T(8,128)} %get-tuple-element.28), channel_id=1, source_target_pairs={{0,16},{16,0},{1,17},{17,1},{2,18},{18,2},{3,19},{19,3},{4,20},{20... | collective-permute-start | bytes 294920 | tf_op jit(solution)/shard_map/ppermute | solution.py:915
  19.9 9.9 %all-gather.1 = f32[1024,128]{1,0:T(8,128)} all-gather(f32[256,128]{1,0:T(8,128)} %get-tuple-element.30), channel_id=3, replica_groups=mesh['x'=4,'yh'=2,'yl'=2,'core'=2,'front'=8] {'yl','core'}, dimensions={0}, use_global_device_ids=true | all-gather | bytes 655360 | tf_op jit(solution)/shard_map/all_gather | solution.py:962
  29.9 0.0 collective-permute-done
  29.9 1.7 pad_maximum_fusion
  31.6 36.7 %all-gather.8.cloned.1.call-done = f32[14336,128]{1,0:T(8,128)} async-done(((f32[896,128]{1,0:T(8,128)}), f32[14336,128]{1,0:T(8,128)}) %all-gather.8.cloned.1.call-update) | async-done | bytes 7340048 | tf_op jit(solution)/shard_map/all_gather | solution.py:945
  68.3 0.0 all-gather.10.cloned.1.call-update
  68.3 0.0 all-gather.12.cloned.1.call-start
  68.3 0.7 all-gather.12.cloned.1.call-update
  69.0 39.5 %chol.1 = (f32[8,1024,128]{2,1,0:T(8,128)}, f32[4,256,256]{2,1,0:T(8,128)}, f32[8,1024,128]{2,1,0:T(8,128)}, f32[36,128,128]{2,1,0:T(8,128)}) custom-call(s32[5]{0:T(128)} %stack.23.ids, s32[16,2,16]{2,1,0:T(2,128)} %block_map.3, f32[16,896,128]{2,1,0:T(8,128)} %bitcast.12), custom_call_target="tpu_custom_call" | custom-call | flops 40000000000 | bytes 100000000 | tf_op jit(solution)/shard_map/chol/pallas_call | solution.py:900
  108.5 8.7 %all-gather.10.cloned.1.call-done = f32[13312,128]{1,0:T(8,128)} async-done(((f32[832,128]{1,0:T(8,128)}), f32[13312,128]{1,0:T(8,128)}) %all-gather.10.cloned.1.call-update) | async-done | bytes 6815760 | tf_op jit(solution)/shard_map/all_gather | solution.py:966
  117.2 20.5 %rest.1 = (f32[1024,128]{1,0:T(8,128)}, f32[11,128,128]{2,1,0:T(8,128)}, f32[11,128,128]{2,1,0:T(8,128)}, f32[14,128,128]{2,1,0:T(8,128)}) custom-call(s32[5]{0:T(128)} %stack.23.ids, s32[8,2,16]{2,1,0:T(2,128)} %map_two.1, f32[8,1024,128]{2,1,0:T(8,128)} %get-tuple-element.32.chol_in, f32[4,256,256]{2,1,0:T(8,128)} %get-tuple-element.33.pairs_in, ...), custom_call_target="tpu_custom_call" | custom-call | flops 15000000512 | bytes 37500000 | tf_op jit(solution)/shard_map/rest/pallas_call | solution.py:900
  137.7 1.3 collective-permute-start.1
  139.0 16.6 %collective-permute-done.1.far_mine = f32[11,128,128]{2,1,0:T(8,128)S(1)} collective-permute-done((f32[11,128,128]{2,1,0:T(8,128)}, f32[11,128,128]{2,1,0:T(8,128)S(1)}, u32[]{:S(2)}, u32[]{:S(2)}) %collective-permute-start.1) | collective-permute-done | bytes 720928 | tf_op jit(solution)/shard_map/ppermute | solution.py:915
  155.6 0.0 copy-start.1
  155.6 1.0 collective-permute-start.2
  156.5 1.2 collective-permute-start.3
  157.7 3.2 %all-gather.12.cloned.1.call-done = f32[10240,128]{1,0:T(8,128)} async-done(((f32[640,128]{1,0:T(8,128)}), f32[10240,128]{1,0:T(8,128)}) %all-gather.12.cloned.1.call-update) | async-done | bytes 5242896 | tf_op jit(solution)/shard_map/all_gather | solution.py:984
  161.0 0.0 collective-permute-done.2.far_other
  161.0 0.0 copy-start.2
  161.0 0.0 copy-done.1
  161.0 0.9 copy-done.2
  161.8 30.8 %chol_two.1 = (f32[8,1024,128]{2,1,0:T(8,128)}, f32[8,128,128]{2,1,0:T(8,128)}) custom-call(s32[5]{0:T(128)} %stack.23.ids, s32[8,2,16]{2,1,0:T(2,128)} %map_two.1, f32[16,640,128]{2,1,0:T(8,128)} %bitcast.9, f32[11,128,128]{2,1,0:T(8,128)} %get-tuple-element.39.near_mine, f32[11,128,128]{2,1,0:T(8,128)} %get-tuple-element.40.near_other, ...), custom_call_target="tpu_custom_call" | custom-call | flops 40000000000 | bytes 100000000 | tf_op jit(solution)/shard_map/chol_two/pallas_call | solution.py:900
  192.7 0.0 collective-permute-done.3.far_late
  192.7 0.0 copy-start
  192.7 0.9 copy-done
  193.6 10.7 %tail.1 = (f32[512,128]{1,0:T(8,128)}, f32[256,128]{1,0:T(8,128)}) custom-call(s32[5]{0:T(128)} %stack.23.ids, s32[8,2,16]{2,1,0:T(2,128)} %map_two.1, f32[16,640,128]{2,1,0:T(8,128)} %bitcast.10, f32[8,1024,128]{2,1,0:T(8,128)} %get-tuple-element.41.chol_in, f32[8,128,128]{2,1,0:T(8,128)} %get-tuple-element.42.inverse_in, f32[4,256,128]{2,1,0:T(8,128)} %bitcast.11, ...), custom_call_target="tpu_custom_call" | custom-call | tf_op jit(solution)/shard_map/tail/pallas_call | solution.py:900
Async XLA Ops:
  7.2 61.1 %all-gather.8.cloned.1.call-start = ((), (), s32[]{:S(2)}) async-start(), calls=%async_computation | async-start | bytes 7798784 | tf_op jit(solution)/shard_map/all_gather | solution.py:945
  12.7 104.5 %all-gather.10.cloned.1.call-start = ((), (), s32[]{:S(2)}) async-start(), calls=%async_computation.1 | async-start | bytes 7241728 | tf_op jit(solution)/shard_map/all_gather | solution.py:966
  17.8 12.1 %collective-permute-start = (f32[192,128]{1,0:T(8,128)}, f32[192,128]{1,0:T(8,128)S(1)}, u32[]{:S(2)}, u32[]{:S(2)}) collective-permute-start(f32[192,128]{1,0:T(8,128)} %get-tuple-element.28), channel_id=1, source_target_pairs={{0,16},{16,0},{1,17},{17,1},{2,18},{18,2},{3,19},{19,3},{4,20},{20... | collective-permute-start | bytes 294920 | tf_op jit(solution)/shard_map/ppermute | solution.py:915
  68.3 92.7 %all-gather.12.cloned.1.call-start = ((), (), s32[]{:S(2)}) async-start(), calls=%async_computation.2 | async-start | bytes 5570560 | tf_op jit(solution)/shard_map/all_gather | solution.py:984
  137.7 17.9 %collective-permute-start.1 = (f32[11,128,128]{2,1,0:T(8,128)}, f32[11,128,128]{2,1,0:T(8,128)S(1)}, u32[]{:S(2)}, u32[]{:S(2)}) collective-permute-start(f32[11,128,128]{2,1,0:T(8,128)} %get-tuple-element.39.near_mine), channel_id=1, source_target_pairs={{0,16},{16,0},{1,17},{17,1},{2,18},{18,2},{3,19},{19,3},{4,20},{20... | collective-permute-start | bytes 2162696 | tf_op jit(solution)/shard_map/ppermute | solution.py:915
  155.6 5.4 %copy-start.1 = (f32[11,128,128]{2,1,0:T(8,128)}, f32[11,128,128]{2,1,0:T(8,128)S(1)}, u32[]{:S(2)}) copy-start(f32[11,128,128]{2,1,0:T(8,128)S(1)} %collective-permute-done.1.far_mine) | copy-start | bytes 2162692
  155.6 5.4 %collective-permute-start.2 = (f32[11,128,128]{2,1,0:T(8,128)S(1)}, f32[11,128,128]{2,1,0:T(8,128)S(1)}, u32[]{:S(2)}, u32[]{:S(2)}) collective-permute-start(f32[11,128,128]{2,1,0:T(8,128)S(1)} %collective-permute-done.1.far_mine), channel_id=1, source_target_pairs={{0,8},{8,0},{1,9},{9,1},{2,10},{10,2},{3,11},{11,3},{4,12},{12,4},... | collective-permute-start | bytes 2162696 | tf_op jit(solution)/shard_map/ppermute | solution.py:915
  156.5 36.1 %collective-permute-start.3 = (f32[14,128,128]{2,1,0:T(8,128)}, f32[14,128,128]{2,1,0:T(8,128)S(1)}, u32[]{:S(2)}, u32[]{:S(2)}) collective-permute-start(f32[14,128,128]{2,1,0:T(8,128)} %get-tuple-element.46.near_late), channel_id=1, source_target_pairs={{0,16},{16,0},{1,17},{17,1},{2,18},{18,2},{3,19},{19,3},{4,20},{20... | collective-permute-start | bytes 2752520 | tf_op jit(solution)/shard_map/ppermute | solution.py:915
  161.0 0.9 copy-start.2
  192.7 0.9 copy-start
Sparse Core Ops, SparseCore 0:
  12.8 55.4 all-gather.7
  70.1 47.0 all-gather.9
  119.0 41.8 all-gather.11
